TPU v7x, 32 devices: a whole 2x2x4 slice. The times are simulated.
32 devices in a mesh: node: 8 (over z, x), rep: 4 (over y, core).
Axes of the slice: x: 2, y: 2, z: 4, core: 2. Of those that a mesh axis runs over, the one named last changes fastest.
Arguments:
- features: bfloat16 [8192, 512], P(('node', 'rep')), may hold values from -6 to 6
- weight: bfloat16 [512, 512], replicated, may hold values from -0.25 to 0.25
- cotangent: bfloat16 [8192, 512], P(('node', 'rep')), may hold values from -6 to 6
- tile_values: bfloat16 [8192, 128, 128], P(('node', 'rep')), may hold values from -0.125 to 0.125
- tile_row: int32 [8192], P(('node', 'rep')), may hold values from 0 to 7
- tile_col: int32 [8192], P(('node', 'rep')), may hold values from 0 to 15
- tile_count: int32 [32], P(('node', 'rep')), may hold values from 64 to 256, as said below
Outputs:
- activation: bfloat16 [8192, 512], P(('node', 'rep'))
- weight_grad: float32 [512, 512], replicated
- feature_grad: bfloat16 [8192, 512], P(('node', 'rep'))
Inputs may be any that keep to these rules, and one draw needn't show every extreme that they name: `tile_count`: slots of a device below its count hold tiles, the others are ignored; some device uses all 256 slots.
All inputs are finite; a program needn't handle non-finite values.
Results may differ from a plain program's by a relative error of at most 0.023.
Values may be sent and summed in bfloat16 or wider, within the bound.
A program may use at most 128 MiB of HBM per device.

v0:
```python
import math

import jax
import jax.numpy as jnp
from jax import lax
from jax.sharding import PartitionSpec as P

TB = 128


def smooth_gate(values):
    return jax.nn.gelu(values, approximate=True)


def apply_tiles(
    tile_values, tile_row, tile_col, tile_count, sources, target_shape, backward, window_start
):
    group_size = min(32, tile_row.shape[0])
    filled = tile_count[0]
    turns_needed = (filled + group_size - 1) // group_size
    window_blocks = target_shape[0]

    def one_turn(turn_index, totals):
        offset = turn_index * group_size
        values = lax.dynamic_slice_in_dim(tile_values, offset, group_size, 0)
        rows_here = lax.dynamic_slice_in_dim(tile_row, offset, group_size, 0)
        cols_here = lax.dynamic_slice_in_dim(tile_col, offset, group_size, 0)
        slot_mask = (offset + jnp.arange(group_size, dtype=jnp.int32) < filled).astype(jnp.float32)
        if backward:
            local_cols = cols_here - window_start
            inside = ((local_cols >= 0) & (local_cols < window_blocks)).astype(jnp.float32)
            placed = jnp.clip(local_cols, 0, window_blocks - 1)
            product = jnp.einsum(
                "tji,tjf->tif", values, sources[rows_here], preferred_element_type=jnp.float32
            )
            return totals.at[placed].add(product * (slot_mask * inside)[:, None, None])
        product = jnp.einsum(
            "tij,tjf->tif", values, sources[cols_here], preferred_element_type=jnp.float32
        )
        return totals.at[rows_here].add(product * slot_mask[:, None, None])

    return lax.fori_loop(0, turns_needed, one_turn, jnp.zeros(target_shape, jnp.float32))


def local(features, weight, cotangent, tile_values, tile_row, tile_col, tile_count):
    rows_quarter = features.shape[0]
    feature_width = features.shape[1]
    rep_count = lax.axis_size("rep")
    node_count = lax.axis_size("node")
    scale = 1.0 / math.sqrt(rows_quarter * rep_count * node_count)
    gathered = lax.all_gather(features, "node", axis=0, tiled=True)
    source_blocks = gathered.reshape(-1, TB, feature_width)
    block_count = rows_quarter * rep_count // TB
    partial_value = apply_tiles(
        tile_values,
        tile_row,
        tile_col,
        tile_count,
        source_blocks,
        (block_count, TB, feature_width),
        False,
        0,
    ).reshape(block_count * TB, feature_width)
    aggregate_all = lax.psum(partial_value, "rep").astype(jnp.bfloat16)
    cotangent_all = lax.all_gather(cotangent, "rep", axis=0, tiled=True)
    pre = jnp.dot(aggregate_all, weight, preferred_element_type=jnp.float32)
    activated, pullback = jax.vjp(smooth_gate, pre)
    grad_all = pullback(cotangent_all.astype(jnp.float32))[0].astype(jnp.bfloat16)
    full_grad = jnp.dot(grad_all, weight.T, preferred_element_type=jnp.float32).astype(jnp.bfloat16)
    offset = lax.axis_index("rep") * rows_quarter
    own_aggregate = lax.dynamic_slice_in_dim(aggregate_all, offset, rows_quarter, 0)
    own_grad = lax.dynamic_slice_in_dim(grad_all, offset, rows_quarter, 0)
    weight_term = jnp.dot(own_aggregate.T, own_grad, preferred_element_type=jnp.float32)
    output_rows = lax.dynamic_slice_in_dim(activated, offset, rows_quarter, 0).astype(jnp.bfloat16)
    weight_grad = lax.psum(weight_term, ("node", "rep")) * scale
    grad_blocks = full_grad.reshape(block_count, TB, feature_width)
    contributions = apply_tiles(
        tile_values, tile_row, tile_col, tile_count, grad_blocks, source_blocks.shape, True, 0
    )
    feature_grad = lax.psum_scatter(
        contributions.reshape(-1, feature_width).astype(jnp.bfloat16),
        "node",
        scatter_dimension=0,
        tiled=True,
    )
    return (output_rows, weight_grad, feature_grad)


def solution(mesh):
    in_specs = (
        P(("node", "rep"), None),
        P(),
        P(("node", "rep"), None),
        P(("node", "rep"), None, None),
        P(("node", "rep")),
        P(("node", "rep")),
        P(("node", "rep")),
    )
    out_specs = (P(("node", "rep"), None), P(), P(("node", "rep"), None))
    return jax.shard_map(local, mesh=mesh, in_specs=in_specs, out_specs=out_specs, check_vma=False)
```

profile of v0, /device:TPU:0, one launch (start us, length us, event | category | flops | bytes accessed | tf_op | source)
XLA Modules:
  0.0 614.2 jit_solution(17007301135434615890)
XLA Ops:
  9.4 52.6 %all-gather.3.cloned.1.call-done = bf16[2048,512]{1,0:T(8,128)(2,1)} async-done(((bf16[256,512]{1,0:T(8,128)(2,1)}), bf16[2048,512]{1,0:T(8,128)(2,1)}) %all-gather.3.cloned.1.call-update) | async-done | bytes 2097168 | tf_op jit(solution)/shard_map/all_gather | solution.py:51
  62.3 72.0 %while.20 = (s32[]{:T(128)}, f32[8,128,512]{2,1,0:T(8,128)S(1)}, s32[]{:T(128)}, s32[256]{0:T(256)S(1)}, bf16[256,128,128]{2,1,0:T(8,128)(2,1)}, /*index=5*/s32[...) while((s32[]{:T(128)}, f32[8,128,512]{2,1,0:T(8,128)S(1)}, ...), condition=%wide.region_2.3_spmd, body=%wide.region_0.2_spmd.sunk | while | flops 541066560 | bytes 47191344 | solution.py:42
  63.0 4.4 gather_fusion
  67.4 7.2 %broadcast_multiply_fusion.5 = f32[32,128,512]{2,1,0:T(8,128)} fusion(f32[32]{0:T(128)S(1)} %compare_convert_fusion.3, bf16[32,128,512]{2,1,0:T(8,128)(2,1)} %gather_fusion, bf16[256,128,128]{2,1,0:T(8,128)(2,1)} %get-tuple-element.274, s32[]{:T(128)S(6)} %select_n.44), kind=kOutput, calls=%fused_computation.4.clone.1 | convolution fusion | flops 538968064 | bytes 13631620 | tf_op jit(solution)/shard_map/while/body/tij,tjf->tif/dot_general | solution.py:37
  74.6 11.8 %scatter_fusion = f32[8,128,512]{2,1,0:T(8,128)S(1)} fusion(f32[8,128,512]{2,1,0:T(8,128)S(1)} %get-tuple-element.259, s32[32]{0:T(128)S(1)} %get-tuple-element.234, f32[32,128,512]{2,1,0:T(8,128)} %broadcast_multiply_fusion.5), kind=kCustom, calls=%fused_computation.2.clone.1 | custom fusion | flops 2097152 | bytes 25165952 | tf_op jit(solution)/shard_map/while/body/scatter-add | solution.py:40
  87.2 4.4 gather_fusion
  91.6 7.0 %broadcast_multiply_fusion.5 = f32[32,128,512]{2,1,0:T(8,128)} fusion(f32[32]{0:T(128)S(1)} %compare_convert_fusion.3, bf16[32,128,512]{2,1,0:T(8,128)(2,1)} %gather_fusion, bf16[256,128,128]{2,1,0:T(8,128)(2,1)} %get-tuple-element.274, s32[]{:T(128)S(6)} %select_n.44), kind=kOutput, calls=%fused_computation.4.clone.1 | convolution fusion | flops 538968064 | bytes 13631620 | tf_op jit(solution)/shard_map/while/body/tij,tjf->tif/dot_general | solution.py:37
  98.5 11.8 %scatter_fusion = f32[8,128,512]{2,1,0:T(8,128)S(1)} fusion(f32[8,128,512]{2,1,0:T(8,128)S(1)} %get-tuple-element.259, s32[32]{0:T(128)S(1)} %get-tuple-element.234, f32[32,128,512]{2,1,0:T(8,128)} %broadcast_multiply_fusion.5), kind=kCustom, calls=%fused_computation.2.clone.1 | custom fusion | flops 2097152 | bytes 25165952 | tf_op jit(solution)/shard_map/while/body/scatter-add | solution.py:40
  111.1 4.4 gather_fusion
  115.5 7.0 %broadcast_multiply_fusion.5 = f32[32,128,512]{2,1,0:T(8,128)} fusion(f32[32]{0:T(128)S(1)} %compare_convert_fusion.3, bf16[32,128,512]{2,1,0:T(8,128)(2,1)} %gather_fusion, bf16[256,128,128]{2,1,0:T(8,128)(2,1)} %get-tuple-element.274, s32[]{:T(128)S(6)} %select_n.44), kind=kOutput, calls=%fused_computation.4.clone.1 | convolution fusion | flops 538968064 | bytes 13631620 | tf_op jit(solution)/shard_map/while/body/tij,tjf->tif/dot_general | solution.py:37
  122.4 11.8 %scatter_fusion = f32[8,128,512]{2,1,0:T(8,128)S(1)} fusion(f32[8,128,512]{2,1,0:T(8,128)S(1)} %get-tuple-element.259, s32[32]{0:T(128)S(1)} %get-tuple-element.234, f32[32,128,512]{2,1,0:T(8,128)} %broadcast_multiply_fusion.5), kind=kCustom, calls=%fused_computation.2.clone.1 | custom fusion | flops 2097152 | bytes 25165952 | tf_op jit(solution)/shard_map/while/body/scatter-add | solution.py:40
  134.2 108.8 %all-reduce.4 = bf16[1024,512]{1,0:T(8,128)(2,1)} all-reduce(f32[1024,512]{1,0:T(8,128)S(1)} %bitcast.16), channel_id=1, replica_groups=mesh['node'=8,'rep'=4] {'rep'}, use_global_device_ids=true, to_apply=%region_3.4 | all-reduce | flops 524288 | bytes 3145728 | tf_op jit(solution)/shard_map/psum | solution.py:64
  243.1 5.3 fusion.6
  254.0 87.7 %while.21 = (s32[]{:T(128)}, f32[16,128,512]{2,1,0:T(8,128)}, s32[]{:T(128)}, s32[256]{0:T(256)S(1)}, bf16[256,128,128]{2,1,0:T(8,128)(2,1)}, /*index=5*/s32[256...) while((s32[]{:T(128)}, f32[16,128,512]{2,1,0:T(8,128)}, ...), condition=%wide.region_7.8_spmd, body=%wide.region_5.7_spmd.sunk | while | flops 541066688 | bytes 47191480 | solution.py:42
  254.8 2.8 gather_fusion.1
  257.5 7.3 %broadcast_multiply_fusion.6 = f32[32,128,512]{2,1,0:T(8,128)} fusion(f32[32]{0:T(128)S(1)} %and_select_fusion.2, bf16[32,128,512]{2,1,0:T(8,128)(2,1)} %gather_fusion.1, bf16[256,128,128]{2,1,0:T(8,128)(2,1)} %get-tuple-element.310, s32[]{:T(128)S(6)} %select_n.46), kind=kOutput, calls=%fused_computation.11.clone.1 | convolution fusion | flops 538968064 | bytes 13631620 | tf_op jit(solution)/shard_map/while/body/tji,tjf->tif/dot_general | solution.py:33
  264.8 18.3 %scatter_fusion.1 = f32[16,128,512]{2,1,0:T(8,128)} fusion(f32[16,128,512]{2,1,0:T(8,128)} %get-tuple-element.295, s32[32]{0:T(128)S(1)} %get-tuple-element.244, f32[32,128,512]{2,1,0:T(8,128)} %broadcast_multiply_fusion.6), kind=kCustom, calls=%fused_computation.3.clone.1 | custom fusion | flops 2097152 | bytes 25165952 | tf_op jit(solution)/shard_map/while/body/scatter-add | solution.py:36
  286.7 7.3 %broadcast_multiply_fusion.6 = f32[32,128,512]{2,1,0:T(8,128)} fusion(f32[32]{0:T(128)S(1)} %and_select_fusion.2, bf16[32,128,512]{2,1,0:T(8,128)(2,1)} %gather_fusion.1, bf16[256,128,128]{2,1,0:T(8,128)(2,1)} %get-tuple-element.310, s32[]{:T(128)S(6)} %select_n.46), kind=kOutput, calls=%fused_computation.11.clone.1 | convolution fusion | flops 538968064 | bytes 13631620 | tf_op jit(solution)/shard_map/while/body/tji,tjf->tif/dot_general | solution.py:33
  294.0 18.4 %scatter_fusion.1 = f32[16,128,512]{2,1,0:T(8,128)} fusion(f32[16,128,512]{2,1,0:T(8,128)} %get-tuple-element.295, s32[32]{0:T(128)S(1)} %get-tuple-element.244, f32[32,128,512]{2,1,0:T(8,128)} %broadcast_multiply_fusion.6), kind=kCustom, calls=%fused_computation.3.clone.1 | custom fusion | flops 2097152 | bytes 25165952 | tf_op jit(solution)/shard_map/while/body/scatter-add | solution.py:36
  316.0 7.3 %broadcast_multiply_fusion.6 = f32[32,128,512]{2,1,0:T(8,128)} fusion(f32[32]{0:T(128)S(1)} %and_select_fusion.2, bf16[32,128,512]{2,1,0:T(8,128)(2,1)} %gather_fusion.1, bf16[256,128,128]{2,1,0:T(8,128)(2,1)} %get-tuple-element.310, s32[]{:T(128)S(6)} %select_n.46), kind=kOutput, calls=%fused_computation.11.clone.1 | convolution fusion | flops 538968064 | bytes 13631620 | tf_op jit(solution)/shard_map/while/body/tji,tjf->tif/dot_general | solution.py:33
  323.3 18.4 %scatter_fusion.1 = f32[16,128,512]{2,1,0:T(8,128)} fusion(f32[16,128,512]{2,1,0:T(8,128)} %get-tuple-element.295, s32[32]{0:T(128)S(1)} %get-tuple-element.244, f32[32,128,512]{2,1,0:T(8,128)} %broadcast_multiply_fusion.6), kind=kCustom, calls=%fused_computation.3.clone.1 | custom fusion | flops 2097152 | bytes 25165952 | tf_op jit(solution)/shard_map/while/body/scatter-add | solution.py:36
  341.7 3.8 convert_element_type.37
  347.5 83.1 %all-reduce.3.cloned.1.call-done = f32[512,512]{1,0:T(8,128)} async-done(((f32[512,512]{1,0:T(8,128)}), f32[512,512]{1,0:T(8,128)}) %all-reduce.3.cloned.1.call-update) | async-done | bytes 1048592 | tf_op jit(solution)/shard_map/psum | solution.py:75
  432.9 174.7 %reduce-scatter.2.cloned.1.call-done = bf16[256,512]{1,0:T(8,128)(2,1)} async-done(((bf16[2048,512]{1,0:T(8,128)(2,1)}), bf16[256,512]{1,0:T(8,128)(2,1)}) %reduce-scatter.2.cloned.1.call-update) | async-done | bytes 262160 | tf_op jit(solution)/shard_map/reduce_scatter | solution.py:80
  (41 shorter events, 21.8 us)
Async XLA Ops:
  7.2 235.9 %copy-start = (bf16[512,512]{1,0:T(8,128)(2,1)S(1)}, bf16[512,512]{1,0:T(8,128)(2,1)}, u32[]{:S(2)}) copy-start(bf16[512,512]{1,0:T(8,128)(2,1)} %param.12) | copy-start | bytes 1572868
  7.2 55.1 %copy-start.1 = (s32[256]{0:T(256)S(1)}, s32[256]{0:T(256)}, u32[]{:S(2)}) copy-start(s32[256]{0:T(256)} %param.16) | copy-start | bytes 3076
  7.2 55.1 %copy-start.2 = (s32[256]{0:T(256)S(1)}, s32[256]{0:T(256)}, u32[]{:S(2)}) copy-start(s32[256]{0:T(256)} %param.15) | copy-start | bytes 3076
  7.2 54.8 %all-gather.3.cloned.1.call-start = ((), (), s32[]{:S(2)}) async-start(), calls=%async_computation.1 | async-start | bytes 2359296 | tf_op jit(solution)/shard_map/all_gather | solution.py:51
  7.9 235.1 %all-gather.5.cloned.1.call-start = ((), (), s32[]{:S(2)}) async-start(), calls=%async_computation.2 | async-start | bytes 1310720 | tf_op jit(solution)/shard_map/all_gather | solution.py:65
  8.7 422.0 %all-reduce.3.cloned.1.call-start = ((), (), s32[]{:S(2)}) async-start(), calls=%async_computation.3 | async-start | bytes 2097152 | tf_op jit(solution)/shard_map/psum | solution.py:75
  251.4 356.3 %reduce-scatter.2.cloned.1.call-start = ((), (), s32[]{:S(2)}) async-start(), calls=%async_computation.4 | async-start | bytes 2359296 | tf_op jit(solution)/shard_map/reduce_scatter | solution.py:80
Sparse Core Ops, SparseCore 0:
  10.1 51.7 all-gather.2
  63.5 15.2 all-gather.4
  251.5 179.0 all-reduce.2
  434.6 173.0 reduce-scatter.1
where the time goes:
time: 616 us; the launch traced here: 614 us
  waiting for transfers between devices  312 us (51%)
  blocking collectives  109 us (18%)
  other arithmetic  103 us (17%)
  matrix products  51.4 us (8%)
  local copies, waits for them, and re-layouts  24.1 us (4%)
  between operations  14.5 us (2%)
    reduce_scatter x1, waiting for transfers between devices, local(): lax.psum_scatter(contributions.reshape(-1, feature_width).astype(jnp.bflo...  175 us
    psum x1, blocking collectives, local(): aggregate_all = lax.psum(partial_value, 'rep').astype(jnp.bfloat16)  109 us
    psum x1, waiting for transfers between devices, local(): weight_grad = lax.psum(weight_term, ('node', 'rep')) * scale  83.1 us
    scatter-add x3, other arithmetic, one_turn(): return totals.at[placed].add(product * (slot_mask * inside)[:, None, None])  55.1 us
    all_gather x1, waiting for transfers between devices, local(): gathered = lax.all_gather(features, 'node', axis=0, tiled=True)  52.6 us
    scatter-add x3, other arithmetic, one_turn(): return totals.at[rows_here].add(product * slot_mask[:, None, None])  35.3 us
    dot_general x3, matrix products, one_turn(): jnp.einsum('tji,tjf->tif', values, sources[rows_here], preferred_element_...  21.9 us
    dot_general x3, matrix products, one_turn(): jnp.einsum('tij,tjf->tif', values, sources[cols_here], preferred_element_...  21.2 us
  transfers between devices with their start and end apart: 4, of which 3 were waited for; matrix products, arithmetic and copies ran while one was open for 28% of the time, Pallas kernels for 0%

commit v1 on v0

v1 whole, which is shorter than its diff:
```python
import functools
import math

import jax
import jax.numpy as jnp
from jax import lax
from jax.experimental import pallas as pl
from jax.experimental.pallas import tpu as pltpu
from jax.sharding import PartitionSpec as P

TB = 128


def densify_kernel(blocks, subs, group, rows_ref, cols_ref, count_ref, tiles_ref, out_ref, acc, stage, sems):
    turn = pl.program_id(0)
    places = acc.shape[0] - 1
    nodes = places // (blocks * subs)

    @pl.when(turn == 0)
    def _():
        @pl.loop(0, places)
        def _(p):
            acc[p] = jnp.zeros((TB, TB), jnp.float32)

    count = count_ref[0]

    @pl.when(turn * group < count)
    def _():
        for t in range(group):
            slot = turn * group + t
            col = cols_ref[slot]
            place = (col // subs * blocks + rows_ref[slot]) * subs + col % subs
            place = jnp.where(slot < count, place, places)
            acc[place] += tiles_ref[t].astype(jnp.float32)

    @pl.when(turn == pl.num_programs(0) - 1)
    def _():
        def copy_out(o):
            return pltpu.make_async_copy(stage.at[o % 2], out_ref.at[o], sems.at[o % 2])

        for o in range(nodes):
            if o >= 2:
                copy_out(o - 2).wait()
            for r in range(blocks):
                for s in range(subs):
                    stage[o % 2, r * TB:(r + 1) * TB, s * TB:(s + 1) * TB] = acc[
                        (o * blocks + r) * subs + s
                    ].astype(jnp.bfloat16)
            copy_out(o).start()
        for o in range(max(nodes - 2, 0), nodes):
            copy_out(o).wait()


def densify(tile_values, tile_row, tile_col, tile_count, nodes, blocks, subs):
    slots = tile_values.shape[0]
    group = 16 if slots % 16 == 0 else 1
    places = nodes * blocks * subs

    def tile_block(i, rows, cols, count):
        return (jnp.minimum(i, (count[0] + group - 1) // group - 1), 0, 0)

    return pl.pallas_call(
        functools.partial(densify_kernel, blocks, subs, group),
        out_shape=jax.ShapeDtypeStruct((nodes, blocks * TB, subs * TB), jnp.bfloat16),
        grid_spec=pltpu.PrefetchScalarGridSpec(
            num_scalar_prefetch=3,
            grid=(slots // group,),
            in_specs=[pl.BlockSpec((group, TB, TB), tile_block)],
            out_specs=pl.BlockSpec(memory_space=pl.ANY),
            scratch_shapes=[
                pltpu.VMEM((places + 1, TB, TB), jnp.float32),
                pltpu.VMEM((2, blocks * TB, subs * TB), jnp.bfloat16),
                pltpu.SemaphoreType.DMA((2,)),
            ],
        ),
        compiler_params=pltpu.CompilerParams(vmem_limit_bytes=60 * 1024 * 1024),
        name="densify",
    )(tile_row, tile_col, tile_count, tile_values)


def local(features, weight, cotangent, tile_values, tile_row, tile_col, tile_count):
    rows_quarter, width = features.shape
    rep_count = lax.axis_size("rep")
    node_count = lax.axis_size("node")
    scale = 1.0 / math.sqrt(rows_quarter * rep_count * node_count)
    subs = rows_quarter // TB
    blocks = subs * rep_count
    dense = densify(tile_values, tile_row, tile_col, tile_count, node_count, blocks, subs)
    gathered = lax.all_gather(features, "node", axis=0, tiled=False)
    partial_sum = lax.dot_general(
        dense, gathered, (((0, 2), (0, 1)), ((), ())), preferred_element_type=jnp.float32
    )
    aggregate = lax.psum_scatter(
        partial_sum.astype(jnp.bfloat16), "rep", scatter_dimension=0, tiled=True
    )
    pre = jnp.dot(aggregate, weight, preferred_element_type=jnp.float32)
    activated, pullback = jax.vjp(functools.partial(jax.nn.gelu, approximate=True), pre)
    pre_grad = pullback(cotangent.astype(jnp.float32))[0].astype(jnp.bfloat16)
    row_grad = jnp.dot(pre_grad, weight.T, preferred_element_type=jnp.float32).astype(jnp.bfloat16)
    all_grad = lax.all_gather(row_grad, "rep", axis=0, tiled=True)
    weight_term = jnp.dot(aggregate.T, pre_grad, preferred_element_type=jnp.float32)
    weight_grad = lax.psum(weight_term, ("node", "rep")) * scale
    terms = lax.dot_general(
        dense, all_grad, (((1,), (0,)), ((), ())), preferred_element_type=jnp.float32
    ).astype(jnp.bfloat16)
    feature_grad = lax.psum_scatter(
        terms.reshape(-1, width), "node", scatter_dimension=0, tiled=True
    )
    return (activated.astype(jnp.bfloat16), weight_grad, feature_grad)


def solution(mesh):
    in_specs = (
        P(("node", "rep"), None),
        P(),
        P(("node", "rep"), None),
        P(("node", "rep"), None, None),
        P(("node", "rep")),
        P(("node", "rep")),
        P(("node", "rep")),
    )
    out_specs = (P(("node", "rep"), None), P(), P(("node", "rep"), None))
    return jax.shard_map(local, mesh=mesh, in_specs=in_specs, out_specs=out_specs, check_vma=False)
```

time: 616 us -> 326 us (0.53)
  blocking collectives: 109 us -> 0 us
  other arithmetic: 103 us -> 2.3 us
  waiting for transfers between devices: 312 us -> 277 us
  matrix products: 51.4 us -> 17.1 us
  local copies, waits for them, and re-layouts: 24.1 us -> 0.02 us
  Pallas kernels: 0 us -> 15.3 us
    psum x1 -> x0, blocking collectives: 109 us -> none  [local(): aggregate_all = lax.psum(partial_value, 'rep').astype(jnp.bfloat16)]
    scatter-add x6 -> x0, other arithmetic: 90.5 us -> none  [the longest x3 55.1 us: one_turn(): return totals.at[placed].add(product * (slot_mask * inside)[:, None, None])]
    reduce_scatter x1 -> x2, waiting for transfers between devices: 175 us -> 92.3 us  [the longest x1 68.9 us: local(): lax.psum_scatter(terms.reshape(-1, width), 'node', scatter_dimension=0, t...]
    psum x1, waiting for transfers between devices: 83.1 us -> 130 us  [local(): weight_grad = lax.psum(weight_term, ('node', 'rep')) * scale]
    dot_general x9 -> x5, matrix products: 51.4 us -> 17.1 us  [the longest x1 6.19 us: local(): lax.dot_general(dense, all_grad, (((1,), (0,)), ((), ())), preferred_elem...]
    gather x6 -> x0, local copies, waits for them, and re-layouts: 21.4 us -> none  [the longest x3 13.1 us: one_turn(): sources[cols_here]]
    pallas_call x0 -> x1, Pallas kernels: none -> 15.3 us  [densify(): pl.pallas_call(functools.partial(densify_kernel, blocks, subs, group), ou...]
    convert_element_type x5 -> x0, other arithmetic: 7.78 us -> none  [the longest x1 3.85 us: local(): contributions.reshape(-1, feature_width).astype(jnp.bfloat16)]
  transfers between devices with their start and end apart: 4 -> 5, of which waited for: 3 -> 5; matrix products, arithmetic and copies ran while one was open for 28% -> 3% of each run, Pallas kernels for 0% -> 5%
where the time goes in v1:
time: 326 us
  waiting for transfers between devices  277 us (85%)
  matrix products  17.1 us (5%)
  Pallas kernels  15.3 us (5%)
  between operations  14.4 us (4%)
    psum x1, waiting for transfers between devices, local(): weight_grad = lax.psum(weight_term, ('node', 'rep')) * scale  130 us
    reduce_scatter x1, waiting for transfers between devices, local(): lax.psum_scatter(terms.reshape(-1, width), 'node', scatter_dimension=0, t...  68.9 us
    all_gather x1, waiting for transfers between devices, local(): gathered = lax.all_gather(features, 'node', axis=0, tiled=False)  38.1 us
    reduce_scatter x1, waiting for transfers between devices, local(): lax.psum_scatter(partial_sum.astype(jnp.bfloat16), 'rep', scatter_dimensi...  23.4 us
    all_gather x1, waiting for transfers between devices, local(): all_grad = lax.all_gather(row_grad, 'rep', axis=0, tiled=True)  15.4 us
    pallas_call x1, Pallas kernels, densify(): pl.pallas_call(functools.partial(densify_kernel, blocks, subs, group), ou...  15.3 us
  transfers between devices with their start and end apart: 5, of which 5 were waited for; matrix products, arithmetic and copies ran while one was open for 3% of the time, Pallas kernels for 5%

profile of v1, /device:TPU:0, one launch (start us, length us, event | category | flops | bytes accessed | tf_op | source)
XLA Modules:
  0.0 326.0 jit_solution(5693229874085195882)
XLA Ops:
  7.2 0.0 copy-start
  7.2 0.0 all-gather.6.cloned.1.call-start
  7.2 0.7 all-gather.6.cloned.1.call-update
  7.9 0.0 reduce-scatter.3.cloned.1.call-start
  8.6 15.3 %densify.1 = bf16[8,1024,256]{2,1,0:T(8,128)(2,1)} custom-call(s32[256]{0:T(256)} %rows_ref.1, s32[256]{0:T(256)} %cols_ref.1, s32[1]{0:T(128)S(6)} %copy.13.count_ref, bf16[256,128,128]{2,1,0:T(8,128)(2,1)} %tiles_ref.1), custom_call_target="tpu_custom_call" | custom-call | tf_op jit(solution)/shard_map/densify/pallas_call | solution.py:62
  23.9 38.1 %all-gather.6.cloned.1.call-done = bf16[2048,512]{1,0:T(8,128)(2,1)} async-done(((bf16[256,512]{1,0:T(8,128)(2,1)}), bf16[2048,512]{1,0:T(8,128)(2,1)}) %all-gather.6.cloned.1.call-update) | async-done | bytes 2097168 | tf_op jit(solution)/shard_map/all_gather | solution.py:89
  62.0 6.2 %bitcast_convert_fusion = bf16[1024,512]{1,0:T(8,128)(2,1)} fusion(bf16[8,1024,256]{2,1,0:T(8,128)(2,1)} %densify.1, bf16[8,256,512]{2,1,0:T(8,128)(2,1)} %bitcast.17), kind=kOutput, calls=%fused_computation | convolution fusion | flops 2148007936 | bytes 7340032 | tf_op jit(solution)/shard_map/dot_general | solution.py:90
  68.2 0.0 reduce-scatter.3.cloned.1.call-update
  68.2 0.0 all-gather.4.cloned.1.call-start
  68.3 23.4 %reduce-scatter.3.cloned.1.call-done = bf16[256,512]{1,0:T(8,128)(2,1)} async-done(((bf16[1024,512]{1,0:T(8,128)(2,1)}), bf16[256,512]{1,0:T(8,128)(2,1)}) %reduce-scatter.3.cloned.1.call-update) | async-done | bytes 262160 | tf_op jit(solution)/shard_map/reduce_scatter | solution.py:93
  91.7 2.4 fusion.3
  94.1 1.0 convolution_convert_fusion.1
  95.1 0.0 all-gather.4.cloned.1.call-update
  95.1 0.0 all-reduce.2.cloned.1.call-start
  95.2 0.0 copy-done.1
  95.2 1.3 fusion.11
  96.5 0.0 all-reduce.2.cloned.1.call-update
  96.5 0.0 reduce-scatter.5.cloned.1.call-start
  96.6 15.4 %all-gather.4.cloned.1.call-done = bf16[1024,512]{1,0:T(8,128)(2,1)} async-done(((bf16[256,512]{1,0:T(8,128)(2,1)}), bf16[1024,512]{1,0:T(8,128)(2,1)}) %all-gather.4.cloned.1.call-update) | async-done | bytes 1048592 | tf_op jit(solution)/shard_map/all_gather | solution.py:100
  112.0 6.2 %convolution_convert_fusion = bf16[8,256,512]{2,1,0:T(8,128)(2,1)} fusion(bf16[8,1024,256]{2,1,0:T(8,128)(2,1)} %densify.1, bf16[1024,512]{1,0:T(8,128)(2,1)} %all-gather.4.cloned.1.call-done), kind=kOutput, calls=%fused_computation.1 | convolution fusion | flops 2148532224 | bytes 7340032 | tf_op jit(solution)/shard_map/dot_general | solution.py:103
  118.2 0.0 reduce-scatter.5.cloned.1.call-update
  118.2 130.0 %all-reduce.2.cloned.1.call-done = f32[512,512]{1,0:T(8,128)} async-done(((f32[512,512]{1,0:T(8,128)}), f32[512,512]{1,0:T(8,128)}) %all-reduce.2.cloned.1.call-update) | async-done | bytes 1048592 | tf_op jit(solution)/shard_map/psum | solution.py:102
  248.3 2.3 broadcast_multiply_fusion
  250.6 68.9 %reduce-scatter.5.cloned.1.call-done = bf16[256,512]{1,0:T(8,128)(2,1)} async-done(((bf16[2048,512]{1,0:T(8,128)(2,1)}), bf16[256,512]{1,0:T(8,128)(2,1)}) %reduce-scatter.5.cloned.1.call-update) | async-done | bytes 262160 | tf_op jit(solution)/shard_map/reduce_scatter | solution.py:106
  (4 shorter events, 0.0 us)
Async XLA Ops:
  7.2 84.5 %copy-start = (bf16[512,512]{1,0:T(8,128)(2,1)S(1)}, bf16[512,512]{1,0:T(8,128)(2,1)}, u32[]{:S(2)}) copy-start(bf16[512,512]{1,0:T(8,128)(2,1)} %param.8) | copy-start | bytes 1572868
  7.2 54.8 %all-gather.6.cloned.1.call-start = ((), (), s32[]{:S(2)}) async-start(), calls=%async_computation.6 | async-start | bytes 2359296 | tf_op jit(solution)/shard_map/all_gather | solution.py:89
  7.9 83.8 %reduce-scatter.3.cloned.1.call-start = ((), (), s32[]{:S(2)}) async-start(), calls=%async_computation.2 | async-start | bytes 1310720 | tf_op jit(solution)/shard_map/reduce_scatter | solution.py:93
  62.0 29.7 %copy-start.2 = (bf16[256,512]{1,0:T(8,128)(2,1)S(1)}, bf16[256,512]{1,0:T(8,128)(2,1)}, u32[]{:S(2)}) copy-start(bf16[256,512]{1,0:T(8,128)(2,1)} %param.9) | copy-start | bytes 786436
  68.2 43.8 %all-gather.4.cloned.1.call-start = ((), (), s32[]{:S(2)}) async-start(), calls=%async_computation.4 | async-start | bytes 1310720 | tf_op jit(solution)/shard_map/all_gather | solution.py:100
  91.7 3.5 %copy-start.1 = (bf16[256,512]{1,0:T(8,128)(2,1)S(1)}, bf16[256,512]{1,0:T(8,128)(2,1)}, u32[]{:S(2)}) copy-start(bf16[256,512]{1,0:T(8,128)(2,1)} %reduce-scatter.3.cloned.1.call-done) | copy-start | bytes 786436
  95.1 153.1 %all-reduce.2.cloned.1.call-start = ((), (), s32[]{:S(2)}) async-start(), calls=%async_computation.3 | async-start | bytes 2097152 | tf_op jit(solution)/shard_map/psum | solution.py:102
  96.5 222.9 %reduce-scatter.5.cloned.1.call-start = ((), (), s32[]{:S(2)}) async-start(), calls=%async_computation.5 | async-start | bytes 2359296 | tf_op jit(solution)/shard_map/reduce_scatter | solution.py:106
Sparse Core Ops, SparseCore 0:
  10.1 51.8 all-gather.5
  68.3 23.3 reduce-scatter.2
  95.3 16.6 all-gather.3
  117.6 130.6 all-reduce.1
  252.2 67.1 reduce-scatter.4

commit v2 on v1

--- a/solution.py
+++ b/solution.py
@@ -78,35 +78,382 @@
     )(tile_row, tile_col, tile_count, tile_values)
 
 
+def layer_kernel(
+    nodes, inner, scale, feat, cot, weight, dense_hbm, act_out, wg_out, fg_out,
+    dense, xbuf, acc, cs, cr, ys, yr, agg, gbuf, wacc, wcs, wcr, wxs, wxr, wys, wyr, wzs, wzr, wfull,
+    bown, xs, xr, zs, zr,
+    dense_sem, ag_send, ag_recv, c_send, c_recv, y_send, y_recv, g_send, g_recv,
+    w_send, w_recv, wz_send, wz_recv, wa_send, wa_recv, x_send, x_recv, z_send, z_recv,
+):
+    line = nodes // inner
+    parts = acc.shape[0]
+    rows, width = feat.shape
+    cols = width // parts
+    node, rep = lax.axis_index("node"), lax.axis_index("rep")
+    z, x = node // inner, node % inner
+    y, c = rep // 2, rep % 2
+    up, down, across = (node + inner, rep), (node - inner, rep), (z * inner + 1 - x, rep)
+    mate, over = (node, y * 2 + 1 - c), (node, (1 - y) * 2 + c)
+    bf16, f32 = jnp.bfloat16, jnp.float32
+
+    def remote(src, dst, send, recv, device):
+        return pltpu.make_async_remote_copy(
+            src_ref=src, dst_ref=dst, send_sem=send, recv_sem=recv,
+            device_id=device, device_id_type=pl.DeviceIdType.MESH,
+        )
+
+    load_dense = pltpu.make_async_copy(dense_hbm, dense, dense_sem)
+    load_dense.start()
+
+    barrier = pltpu.get_barrier_semaphore()
+    for device in (across, mate, over):
+        pl.semaphore_signal(barrier, inc=1, device_id=device, device_id_type=pl.DeviceIdType.MESH)
+    for k in range(1, line):
+        pl.semaphore_signal(
+            barrier, inc=1, device_id=((z + k) % line * inner + x, rep),
+            device_id_type=pl.DeviceIdType.MESH,
+        )
+    pl.semaphore_wait(barrier, 3 + line - 1)
+
+    def ag_copy(way, zz, s, src=None):
+        slot = zz * inner + x
+        src = xbuf.at[slot, s] if src is None else src
+        return remote(
+            src, xbuf.at[slot, s], ag_send.at[way, zz, s], ag_recv.at[slot, s], (up, down, across)[way]
+        )
+
+    def ag_wait(slot, s):
+        remote(xbuf.at[slot, s], xbuf.at[slot, s], ag_send.at[0, 0, s], ag_recv.at[slot, s], across).wait_recv()
+
+    for s in range(parts):
+        own = feat.at[:, s * cols:(s + 1) * cols]
+        ag_copy(2, z, s, own).start()
+        pl.when(z < line - 1)(lambda own=own, s=s: ag_copy(0, z, s, own).start())
+        pl.when(z > 0)(lambda own=own, s=s: ag_copy(1, z, s, own).start())
+
+    load_dense.wait()
+    chunk = rows
+
+    def multiply(slot, s, block, first=False):
+        @pl.loop(0, acc.shape[1] // chunk)
+        def _(i):
+            here = pl.ds(pl.multiple_of(i * chunk, chunk), chunk)
+            term = jnp.dot(dense[slot, here, :], block[...], preferred_element_type=f32)
+            if first:
+                acc[s, here, :] = term
+            else:
+                acc[s, here, :] += term
+
+    for s in range(parts):
+        multiply(node, s, feat.at[:, s * cols:(s + 1) * cols], True)
+
+    @pl.loop(1, line)
+    def _(d):
+        low, high = z - d, z + d
+        for s in range(parts):
+            @pl.when(low >= 0)
+            def _():
+                ag_wait(low * inner + x, s)
+                pl.when(z < line - 1)(lambda: ag_copy(0, low, s).start())
+                ag_copy(2, low, s).start()
+
+            @pl.when(high < line)
+            def _():
+                ag_wait(high * inner + x, s)
+                pl.when(z > 0)(lambda: ag_copy(1, high, s).start())
+                ag_copy(2, high, s).start()
+
+        for zz, there in ((low, low >= 0), (high, high < line)):
+            @pl.when(there)
+            def _():
+                for s in range(parts):
+                    multiply(zz * inner + x, s, xbuf.at[zz * inner + x, s])
+
+    @pl.loop(0, line)
+    def _(d):
+        low, high = z - d, z + d
+        for zz, there in ((low, low >= 0), (high, (high < line) & (d > 0))):
+            @pl.when(there)
+            def _():
+                slot = zz * inner + 1 - x
+                for s in range(parts):
+                    ag_wait(slot, s)
+                    multiply(slot, s, xbuf.at[slot, s])
+
+    def quarter(q):
+        return pl.ds(pl.multiple_of(q * rows, rows), rows)
+
+    def c_copy(qy, s):
+        return remote(cs.at[qy, s], cr.at[qy, s], c_send.at[qy, s], c_recv.at[qy, s], mate)
+
+    def y_copy(s):
+        return remote(ys.at[s], yr.at[s], y_send.at[s], y_recv.at[s], over)
+
+    for qy in (1 - y, y):
+        for s in range(parts):
+            cs[qy, s] = acc[s, quarter(qy * 2 + 1 - c), :].astype(bf16)
+            c_copy(qy, s).start()
+    for s in range(parts):
+        c_copy(1 - y, s).wait_recv()
+        ys[s] = (acc[s, quarter((1 - y) * 2 + c), :] + cr[1 - y, s].astype(f32)).astype(bf16)
+        y_copy(s).start()
+    for s in range(parts):
+        c_copy(y, s).wait_recv()
+        y_copy(s).wait_recv()
+        total = acc[s, quarter(rep), :] + cr[y, s].astype(f32) + yr[s].astype(f32)
+        agg[:, s * cols:(s + 1) * cols] = total.astype(bf16)
+
+    pre = jnp.dot(agg[...], weight[...], preferred_element_type=f32)
+    root = math.sqrt(2.0 / math.pi)
+    bend = jnp.tanh(root * (pre + 0.044715 * pre * pre * pre))
+    act_out[...] = (0.5 * pre * (1.0 + bend)).astype(bf16)
+    slope = 0.5 * (1.0 + bend) + 0.5 * pre * (1.0 - bend * bend) * (
+        root * (1.0 + 3 * 0.044715 * pre * pre)
+    )
+    pre_grad = (cot[...].astype(f32) * slope).astype(bf16)
+    row_grad = lax.dot_general(
+        pre_grad, weight[...], (((1,), (1,)), ((), ())), preferred_element_type=f32
+    )
+    gbuf[quarter(rep), :] = row_grad.astype(bf16)
+
+    def g_copy(way, q):
+        here = gbuf.at[quarter(q), :]
+        return remote(here, here, g_send.at[way], g_recv.at[q], (over, mate, mate)[way])
+
+    g_copy(0, rep).start()
+    g_copy(1, rep).start()
+    wacc[...] = lax.dot_general(
+        agg[...], pre_grad, (((0,), (0,)), ((), ())), preferred_element_type=f32
+    )
+    half = wacc.shape[0] // 2
+    fold = half // 2
+
+    def w_copy(step):
+        src, dst, device = (
+            (wcs, wcr, mate), (wxs, wxr, across), (wys, wyr, over),
+            (wfull.at[c, y], wfull.at[c, y], over), (wfull.at[c], wfull.at[c], mate),
+        )[step]
+        return remote(src, dst, w_send.at[step], w_recv.at[step], device)
+
+    def w_arrival(step):
+        dst = (wcr, wxr, wyr, wfull.at[c, 1 - y], wfull.at[1 - c])[step]
+        remote(dst, dst, w_send.at[step], w_recv.at[step], mate).wait_recv()
+
+    def part_of(i, size):
+        return pl.ds(pl.multiple_of(i * size, size), size)
+
+    wcs[...] = wacc[part_of(1 - c, half), :].astype(bf16)
+    w_copy(0).start()
+    w_arrival(0)
+    wxs[...] = (wacc[part_of(c, half), :] + wcr[...].astype(f32)).astype(bf16)
+    w_copy(1).start()
+    g_copy(1, y * 2 + 1 - c).wait_recv()
+    g_copy(0, (1 - y) * 2 + c).wait_recv()
+    g_copy(2, (1 - y) * 2 + c).start()
+    w_arrival(1)
+    wys[...] = (
+        wxs[part_of(1 - y, fold), :].astype(f32) + wxr[part_of(1 - y, fold), :].astype(f32)
+    ).astype(bf16)
+    w_copy(2).start()
+    g_copy(2, (1 - y) * 2 + 1 - c).wait_recv()
+
+    def term_of(slot):
+        return lax.dot_general(
+            dense[slot], gbuf[...], (((0,), (0,)), ((), ())), preferred_element_type=f32
+        )
+
+    def x_copy(zz, s):
+        return remote(xs.at[zz, s], xr.at[zz, s], x_send.at[zz, s], x_recv.at[zz, s], across)
+
+    @pl.loop(0, line)
+    def _(i):
+        d = line - 1 - i
+        for zz, there in ((z + d, z + d < line), (z - d, (z - d >= 0) & (d > 0))):
+            @pl.when(there)
+            def _():
+                term = term_of(zz * inner + 1 - x)
+                for s in range(parts):
+                    xs[zz, s] = term[:, s * cols:(s + 1) * cols].astype(bf16)
+                    x_copy(zz, s).start()
+
+    w_arrival(2)
+    piece = fold // line
+    kept = (
+        wxs[part_of(y, fold), :].astype(f32) + wxr[part_of(y, fold), :].astype(f32)
+        + wyr[...].astype(f32)
+    )
+    wzs[...] = kept.reshape(line, piece, width).astype(bf16)
+
+    def wz_copy(k):
+        other = (z + k) % line
+        return remote(
+            wzs.at[other], wzr.at[z], wz_send.at[k], wz_recv.at[z], (other * inner + x, rep)
+        )
+
+    def wz_wait(k):
+        other = (z + k) % line
+        remote(wzr.at[other], wzr.at[other], wz_send.at[k], wz_recv.at[other], across).wait_recv()
+
+    def wa_copy(k):
+        other = (z + k) % line
+        here = wfull.at[c, y, z]
+        return remote(here, here, wa_send.at[k], wa_recv.at[z], (other * inner + x, rep))
+
+    def wa_wait(k):
+        other = (z + k) % line
+        there = wfull.at[c, y, other]
+        remote(there, there, wa_send.at[k], wa_recv.at[other], across).wait_recv()
+
+    for k in range(1, line):
+        wz_copy(k).start()
+
+    @pl.loop(0, line)
+    def _(zz):
+        term = term_of(zz * inner + x)
+        for s in range(parts):
+            bown[zz, s] = term[:, s * cols:(s + 1) * cols]
+
+    def z_copy(zz, s, slot, device):
+        return remote(zs.at[zz, s], zr.at[slot, s], z_send.at[zz, s], z_recv.at[slot, s], device)
+
+    def z_wait(slot, s):
+        remote(zr.at[slot, s], zr.at[slot, s], z_send.at[0, s], z_recv.at[slot, s], across).wait_recv()
+
+    def pass_on(i):
+        d = line - 1 - i
+        for zz, there, inflow, device, slot in (
+            (z + d, z + d < line, z > 0, up, z + d),
+            (z - d, z - d >= 0, z < line - 1, down, jnp.where(d == 1, line, z - d)),
+        ):
+            @pl.when(there)
+            def _():
+                for s in range(parts):
+                    x_copy(zz, s).wait_recv()
+                    bown[zz, s] += xr[zz, s].astype(f32)
+
+                    @pl.when(inflow)
+                    def _():
+                        z_wait(zz, s)
+                        bown[zz, s] += zr[zz, s].astype(f32)
+
+                    zs[zz, s] = bown[zz, s].astype(bf16)
+                    z_copy(zz, s, slot, device).start()
+
+    pass_on(0)
+    for k in range(1, line):
+        wz_wait(k)
+    piece_sum = wzs[z].astype(f32)
+    for k in range(1, line):
+        piece_sum += wzr[(z + k) % line].astype(f32)
+    wfull[c, y, z] = (piece_sum * scale).astype(bf16)
+    for k in range(1, line):
+        wa_copy(k).start()
+
+    @pl.loop(1, line - 1)
+    def _(i):
+        pass_on(i)
+
+    for k in range(1, line):
+        wa_wait(k)
+    w_copy(3).start()
+    for s in range(parts):
+        x_copy(z, s).wait_recv()
+        bown[z, s] += xr[z, s].astype(f32)
+    w_arrival(3)
+    w_copy(4).start()
+    for s in range(parts):
+        @pl.when(z > 0)
+        def _():
+            z_wait(z, s)
+            bown[z, s] += zr[z, s].astype(f32)
+
+        @pl.when(z < line - 1)
+        def _():
+            z_wait(line, s)
+            bown[z, s] += zr[line, s].astype(f32)
+
+        fg_out[:, s * cols:(s + 1) * cols] = bown[z, s].astype(bf16)
+    w_arrival(4)
+    wg_out[...] = wfull[...].astype(f32)
+
+    @pl.loop(0, line)
+    def _(zz):
+        for s in range(parts):
+            pl.when((zz <= z) & (z < line - 1))(lambda: ag_copy(0, zz, s).wait_send())
+            pl.when((zz >= z) & (z > 0))(lambda: ag_copy(1, zz, s).wait_send())
+            ag_copy(2, zz, s).wait_send()
+            x_copy(zz, s).wait_send()
+            pl.when(zz != z)(lambda: z_copy(zz, s, zz, across).wait_send())
+    for s in range(parts):
+        y_copy(s).wait_send()
+        for qy in range(2):
+            c_copy(qy, s).wait_send()
+    for way in range(3):
+        g_copy(way, rep).wait_send()
+    for step in range(5):
+        w_copy(step).wait_send()
+    for k in range(1, line):
+        wz_copy(k).wait_send()
+        wa_copy(k).wait_send()
+
+
+def layer(features, cotangent, weight, dense, scale, nodes):
+    rows, width = features.shape
+    inner = 2
+    line = nodes // inner
+    parts = 2
+    cols = width // parts
+    all_rows = dense.shape[1]
+    half = width // 2
+    fold = half // 2
+    bf16, f32, dma = jnp.bfloat16, jnp.float32, pltpu.SemaphoreType.DMA
+    vmem = pl.BlockSpec(memory_space=pltpu.VMEM)
+    shapes = [
+        (dense.shape, bf16), ((nodes, parts, rows, cols), bf16), ((parts, all_rows, cols), f32),
+        ((2, parts, rows, cols), bf16), ((2, parts, rows, cols), bf16),
+        ((parts, rows, cols), bf16), ((parts, rows, cols), bf16),
+        ((rows, width), bf16), ((all_rows, width), bf16), ((width, width), f32),
+        ((half, width), bf16), ((half, width), bf16), ((half, width), bf16), ((half, width), bf16),
+        ((fold, width), bf16), ((fold, width), bf16),
+        ((line, fold // line, width), bf16), ((line, fold // line, width), bf16),
+        ((2, 2, line, fold // line, width), bf16),
+        ((line, parts, rows, cols), f32), ((line, parts, rows, cols), bf16),
+        ((line, parts, rows, cols), bf16), ((line, parts, rows, cols), bf16),
+        ((line + 1, parts, rows, cols), bf16),
+    ]
+    sems = [
+        dma, dma((3, line, parts)), dma((nodes, parts)), dma((2, parts)), dma((2, parts)),
+        dma((parts,)), dma((parts,)), dma((3,)), dma((4,)), dma((5,)), dma((5,)),
+        dma((line,)), dma((line,)), dma((line,)), dma((line,)),
+        dma((line, parts)), dma((line, parts)), dma((line, parts)), dma((line + 1, parts)),
+    ]
+    activation, weight_grad, feature_grad = pl.pallas_call(
+        functools.partial(layer_kernel, nodes, inner, scale),
+        out_shape=(
+            jax.ShapeDtypeStruct((rows, width), bf16),
+            jax.ShapeDtypeStruct((2, 2, line, fold // line, width), f32),
+            jax.ShapeDtypeStruct((rows, width), bf16),
+        ),
+        in_specs=[vmem, vmem, vmem, pl.BlockSpec(memory_space=pl.ANY)],
+        out_specs=(vmem, vmem, vmem),
+        scratch_shapes=[pltpu.VMEM(*shape) for shape in shapes] + sems,
+        compiler_params=pltpu.CompilerParams(
+            collective_id=0, has_side_effects=True, vmem_limit_bytes=63 * 1024 * 1024
+        ),
+        name="layer",
+    )(features, cotangent, weight, dense)
+    return activation, weight_grad.reshape(width, width), feature_grad
+
+
 def local(features, weight, cotangent, tile_values, tile_row, tile_col, tile_count):
-    rows_quarter, width = features.shape
+    rows_quarter = features.shape[0]
     rep_count = lax.axis_size("rep")
     node_count = lax.axis_size("node")
     scale = 1.0 / math.sqrt(rows_quarter * rep_count * node_count)
     subs = rows_quarter // TB
     blocks = subs * rep_count
     dense = densify(tile_values, tile_row, tile_col, tile_count, node_count, blocks, subs)
-    gathered = lax.all_gather(features, "node", axis=0, tiled=False)
-    partial_sum = lax.dot_general(
-        dense, gathered, (((0, 2), (0, 1)), ((), ())), preferred_element_type=jnp.float32
-    )
-    aggregate = lax.psum_scatter(
-        partial_sum.astype(jnp.bfloat16), "rep", scatter_dimension=0, tiled=True
-    )
-    pre = jnp.dot(aggregate, weight, preferred_element_type=jnp.float32)
-    activated, pullback = jax.vjp(functools.partial(jax.nn.gelu, approximate=True), pre)
-    pre_grad = pullback(cotangent.astype(jnp.float32))[0].astype(jnp.bfloat16)
-    row_grad = jnp.dot(pre_grad, weight.T, preferred_element_type=jnp.float32).astype(jnp.bfloat16)
-    all_grad = lax.all_gather(row_grad, "rep", axis=0, tiled=True)
-    weight_term = jnp.dot(aggregate.T, pre_grad, preferred_element_type=jnp.float32)
-    weight_grad = lax.psum(weight_term, ("node", "rep")) * scale
-    terms = lax.dot_general(
-        dense, all_grad, (((1,), (0,)), ((), ())), preferred_element_type=jnp.float32
-    ).astype(jnp.bfloat16)
-    feature_grad = lax.psum_scatter(
-        terms.reshape(-1, width), "node", scatter_dimension=0, tiled=True
-    )
-    return (activated.astype(jnp.bfloat16), weight_grad, feature_grad)
+    return layer(features, cotangent, weight, dense, scale, node_count)
 
 
 def solution(mesh):

time: 326 us -> 101 us (0.31)
  waiting for transfers between devices: 277 us -> 0 us
  Pallas kernels: 15.3 us -> 93.5 us
  matrix products: 17.1 us -> 0 us
  between operations: 14.4 us -> 1.29 us
  local copies, waits for them, and re-layouts: 0.02 us -> 5.6 us
    psum x1 -> x0, waiting for transfers between devices: 130 us -> none  [local(): weight_grad = lax.psum(weight_term, ('node', 'rep')) * scale]
    reduce_scatter x2 -> x0, waiting for transfers between devices: 92.3 us -> none  [the longest x1 68.9 us: local(): lax.psum_scatter(terms.reshape(-1, width), 'node', scatter_dimension=0, t...]
    pallas_call x0 -> x1, Pallas kernels: none -> 84.3 us  [layer(): pl.pallas_call(functools.partial(layer_kernel, nodes, inner, scale), out_...]
    all_gather x2 -> x0, waiting for transfers between devices: 53.6 us -> none  [the longest x1 38.1 us: local(): gathered = lax.all_gather(features, 'node', axis=0, tiled=False)]
    dot_general x5 -> x0, matrix products: 17.1 us -> none  [the longest x1 6.19 us: local(): lax.dot_general(dense, all_grad, (((1,), (0,)), ((), ())), preferred_elem...]
    pallas_call x1, Pallas kernels: 15.3 us -> 9.19 us  [densify(): pl.pallas_call(functools.partial(densify_kernel, blocks, subs, group), ou...]
    unnamed x6 -> x3, local copies, waits for them, and re-layouts: 0.02 us -> 5.6 us
  transfers between devices with their start and end apart: 5 -> 0, of which waited for: 5 -> 0; matrix products, arithmetic and copies ran while one was open for 3% -> 0% of each run, Pallas kernels for 5% -> 0%
where the time goes in v2:
time: 101 us; the launch traced here: 100 us
  Pallas kernels  93.5 us (93%)
  local copies, waits for them, and re-layouts  5.6 us (6%)
  between operations  1.29 us (1%)
    pallas_call x1, Pallas kernels, layer(): pl.pallas_call(functools.partial(layer_kernel, nodes, inner, scale), out_...  84.3 us
    pallas_call x1, Pallas kernels, densify(): pl.pallas_call(functools.partial(densify_kernel, blocks, subs, group), ou...  9.19 us
    unnamed x3, local copies, waits for them, and re-layouts  5.6 us

profile of v2, /device:TPU:0, one launch (start us, length us, event | category | flops | bytes accessed | tf_op | source)
XLA Modules:
  0.0 100.4 jit_solution(957229513807938416)
XLA Ops:
  1.3 9.2 %densify.1.dense_hbm = bf16[8,1024,256]{2,1,0:T(8,128)(2,1)} custom-call(s32[256]{0:T(256)} %rows_ref.1, s32[256]{0:T(256)} %cols_ref.1, s32[1]{0:T(128)S(6)} %copy.13.count_ref, bf16[256,128,128]{2,1,0:T(8,128)(2,1)} %tiles_ref.1), custom_call_target="tpu_custom_call" | custom-call | tf_op jit(solution)/shard_map/densify/pallas_call | solution.py:62
  10.5 84.3 %layer.1 = (bf16[256,512]{1,0:T(8,128)(2,1)}, f32[2,2,4,32,512]{4,3,2,1,0:T(8,128)}, bf16[256,512]{1,0:T(8,128)(2,1)}) custom-call(bf16[256,512]{1,0:T(8,128)(2,1)} %feat.1, bf16[256,512]{1,0:T(8,128)(2,1)} %cot.1, bf16[512,512]{1,0:T(8,128)(2,1)} %weight.1, bf16[8,1024,256]{2,1,0:T(8,128)(2,1)} %densify.1.dense_hbm), custom_call_target="tpu_custom_call" | custom-call | tf_op jit(solution)/shard_map/layer/pallas_call | solution.py:430
  94.8 1.7 %copy.14 = bf16[256,512]{1,0:T(8,128)(2,1)} copy(bf16[256,512]{1,0:T(8,128)(2,1)} %get-tuple-element.12) | data formatting | bytes 524288
  96.4 2.3 %copy.15 = f32[512,512]{1,0:T(8,128)} copy(f32[512,512]{1,0:T(8,128)} %bitcast.1) | data formatting | bytes 2097152
  98.7 1.7 %copy.16 = bf16[256,512]{1,0:T(8,128)(2,1)} copy(bf16[256,512]{1,0:T(8,128)(2,1)} %get-tuple-element.14) | data formatting | bytes 524288

commit v3 on v2

v3 whole, which is shorter than its diff:
```python
import functools
import math

import jax
import jax.numpy as jnp
from jax import lax
from jax.experimental import pallas as pl
from jax.experimental.pallas import tpu as pltpu
from jax.sharding import PartitionSpec as P

TB = 128


def densify_kernel(blocks, subs, group, rows_ref, cols_ref, count_ref, tiles_ref, out_ref, acc, stage, sems):
    turn = pl.program_id(0)
    places = acc.shape[0] - 1
    nodes = places // (blocks * subs)

    @pl.when(turn == 0)
    def _():
        @pl.loop(0, places)
        def _(p):
            acc[p] = jnp.zeros((TB, TB), jnp.float32)

    count = count_ref[0]

    @pl.when(turn * group < count)
    def _():
        @pl.loop(0, group, unroll=True)
        def _(t):
            slot = turn * group + t
            col = cols_ref[slot]
            place = (col // subs * blocks + rows_ref[slot]) * subs + col % subs
            place = jnp.where(slot < count, place, places)
            acc[place] += tiles_ref[t].astype(jnp.float32)

    @pl.when(turn == pl.num_programs(0) - 1)
    def _():
        def copy_out(o):
            return pltpu.make_async_copy(stage.at[o % 2], out_ref.at[o], sems.at[o % 2])

        for o in range(nodes):
            if o >= 2:
                copy_out(o - 2).wait()
            for r in range(blocks):
                for s in range(subs):
                    stage[o % 2, r * TB:(r + 1) * TB, s * TB:(s + 1) * TB] = acc[
                        (o * blocks + r) * subs + s
                    ].astype(jnp.bfloat16)
            copy_out(o).start()
        for o in range(max(nodes - 2, 0), nodes):
            copy_out(o).wait()


def densify(tile_values, tile_row, tile_col, tile_count, nodes, blocks, subs):
    slots = tile_values.shape[0]
    group = math.gcd(slots, 32)
    places = nodes * blocks * subs

    def tile_block(i, rows, cols, count):
        return (jnp.minimum(i, (count[0] + group - 1) // group - 1), 0, 0)

    return pl.pallas_call(
        functools.partial(densify_kernel, blocks, subs, group),
        out_shape=jax.ShapeDtypeStruct((nodes, blocks * TB, subs * TB), jnp.bfloat16),
        grid_spec=pltpu.PrefetchScalarGridSpec(
            num_scalar_prefetch=3,
            grid=(slots // group,),
            in_specs=[pl.BlockSpec((group, TB, TB), tile_block)],
            out_specs=pl.BlockSpec(memory_space=pl.ANY),
            scratch_shapes=[
                pltpu.VMEM((places + 1, TB, TB), jnp.float32),
                pltpu.VMEM((2, blocks * TB, subs * TB), jnp.bfloat16),
                pltpu.SemaphoreType.DMA((2,)),
            ],
        ),
        compiler_params=pltpu.CompilerParams(vmem_limit_bytes=60 * 1024 * 1024),
        cost_estimate=pl.CostEstimate(
            flops=slots * TB * TB, bytes_accessed=4 * slots * TB * TB, transcendentals=0
        ),
        name="densify",
    )(tile_row, tile_col, tile_count, tile_values)


def layer_kernel(
    nodes, inner, scale, feat, feat_x, feat_low, feat_high, cot, weight, dense_hbm, act_out, wg_out, fg_out,
    dense, xbuf, acc, cs, cr, ys, yr, agg, gbuf, wacc, wcs, wcr, wxs, wxr, wys, wyr, wzs, wzr, wfull,
    bown, xs, xr, zs, zr,
    dense_sem, ag_send, ag_recv, c_send, c_recv, y_send, y_recv, g_send, g_recv,
    w_send, w_recv, wz_send, wz_recv, wa_send, wa_recv, x_send, x_recv, z_send, z_recv,
):
    line = nodes // inner
    parts = acc.shape[0]
    rows, width = feat.shape
    cols = width // parts
    node, rep = lax.axis_index("node"), lax.axis_index("rep")
    z, x = node // inner, node % inner
    y, c = rep // 2, rep % 2
    up, down, across = (node + inner, rep), (node - inner, rep), (z * inner + 1 - x, rep)
    mate, over = (node, y * 2 + 1 - c), (node, (1 - y) * 2 + c)
    bf16, f32 = jnp.bfloat16, jnp.float32

    def remote(src, dst, send, recv, device):
        return pltpu.make_async_remote_copy(
            src_ref=src, dst_ref=dst, send_sem=send, recv_sem=recv,
            device_id=device, device_id_type=pl.DeviceIdType.MESH,
        )

    load_dense = pltpu.make_async_copy(dense_hbm, dense, dense_sem)
    load_dense.start()

    barrier = pltpu.get_barrier_semaphore()
    for device in (across, mate, over):
        pl.semaphore_signal(barrier, inc=1, device_id=device, device_id_type=pl.DeviceIdType.MESH)
    for k in range(1, line):
        pl.semaphore_signal(
            barrier, inc=1, device_id=((z + k) % line * inner + x, rep),
            device_id_type=pl.DeviceIdType.MESH,
        )
    pl.semaphore_wait(barrier, 3 + line - 1)

    def ag_copy(way, zz, s, src=None):
        slot = zz * inner + x
        src = xbuf.at[slot, s] if src is None else src
        return remote(
            src, xbuf.at[slot, s], ag_send.at[way, zz, s], ag_recv.at[slot, s], (up, down, across)[way]
        )

    def ag_wait(slot, s):
        remote(xbuf.at[slot, s], xbuf.at[slot, s], ag_send.at[0, 0, s], ag_recv.at[slot, s], across).wait_recv()

    def columns(ref, s):
        return ref.at[:, s * cols:(s + 1) * cols]

    for s in range(parts):
        low_part, high_part = columns(feat_low, s), columns(feat_high, s)

        @pl.when(z > 0)
        def _():
            pl.when(z < line - 1)(lambda: ag_copy(0, z - 1, s, low_part).start())
            ag_copy(2, z - 1, s, low_part).start()

        @pl.when(z < line - 1)
        def _():
            pl.when(z > 0)(lambda: ag_copy(1, z + 1, s, high_part).start())
            ag_copy(2, z + 1, s, high_part).start()

    load_dense.wait()
    chunk = rows

    def multiply(slot, s, block, first=False):
        @pl.loop(0, acc.shape[1] // chunk)
        def _(i):
            here = pl.ds(pl.multiple_of(i * chunk, chunk), chunk)
            term = jnp.dot(dense[slot, here, :], block[...], preferred_element_type=f32)
            if first:
                acc[s, here, :] = term
            else:
                acc[s, here, :] += term

    for s in range(parts):
        multiply(node, s, columns(feat, s), True)
        multiply(z * inner + 1 - x, s, columns(feat_x, s))
        pl.when(z > 0)(lambda s=s: multiply(node - inner, s, columns(feat_low, s)))
        pl.when(z < line - 1)(lambda s=s: multiply(node + inner, s, columns(feat_high, s)))

    @pl.loop(2, line)
    def _(d):
        low, high = z - d, z + d
        for s in range(parts):
            @pl.when(low >= 0)
            def _():
                ag_wait(low * inner + x, s)
                pl.when(z < line - 1)(lambda: ag_copy(0, low, s).start())
                ag_copy(2, low, s).start()

            @pl.when(high < line)
            def _():
                ag_wait(high * inner + x, s)
                pl.when(z > 0)(lambda: ag_copy(1, high, s).start())
                ag_copy(2, high, s).start()

        for zz, there in ((low, low >= 0), (high, high < line)):
            @pl.when(there)
            def _():
                for s in range(parts):
                    multiply(zz * inner + x, s, xbuf.at[zz * inner + x, s])

    def multiply_across(d, s):
        for zz, there in ((z - d, z - d >= 0), (z + d, z + d < line)):
            @pl.when(there)
            def _():
                slot = zz * inner + 1 - x
                ag_wait(slot, s)
                multiply(slot, s, xbuf.at[slot, s])

    @pl.loop(1, line - 1)
    def _(d):
        for s in range(parts):
            multiply_across(d, s)

    def quarter(q):
        return pl.ds(pl.multiple_of(q * rows, rows), rows)

    def c_copy(qy, s):
        return remote(cs.at[qy, s], cr.at[qy, s], c_send.at[qy, s], c_recv.at[qy, s], mate)

    def y_copy(s):
        return remote(ys.at[s], yr.at[s], y_send.at[s], y_recv.at[s], over)

    for s in range(parts):
        multiply_across(line - 1, s)
        for qy in (1 - y, y):
            cs[qy, s] = acc[s, quarter(qy * 2 + 1 - c), :].astype(bf16)
            c_copy(qy, s).start()
        c_copy(1 - y, s).wait_recv()
        ys[s] = (acc[s, quarter((1 - y) * 2 + c), :] + cr[1 - y, s].astype(f32)).astype(bf16)
        y_copy(s).start()
    for s in range(parts):
        c_copy(y, s).wait_recv()
        y_copy(s).wait_recv()
        total = acc[s, quarter(rep), :] + cr[y, s].astype(f32) + yr[s].astype(f32)
        agg[:, s * cols:(s + 1) * cols] = total.astype(bf16)

    pre = jnp.dot(agg[...], weight[...], preferred_element_type=f32)
    root = math.sqrt(2.0 / math.pi)
    bend = jnp.tanh(root * (pre + 0.044715 * pre * pre * pre))
    act_out[...] = (0.5 * pre * (1.0 + bend)).astype(bf16)
    slope = 0.5 * (1.0 + bend) + 0.5 * pre * (1.0 - bend * bend) * (
        root * (1.0 + 3 * 0.044715 * pre * pre)
    )
    pre_grad = (cot[...].astype(f32) * slope).astype(bf16)
    row_grad = lax.dot_general(
        pre_grad, weight[...], (((1,), (1,)), ((), ())), preferred_element_type=f32
    )
    for s in range(parts):
        gbuf[s, quarter(rep), :] = row_grad[:, s * cols:(s + 1) * cols].astype(bf16)

    def g_copy(way, q, s):
        here = gbuf.at[s, quarter(q), :]
        return remote(here, here, g_send.at[way, s], g_recv.at[q, s], (over, mate, mate)[way])

    for s in range(parts):
        g_copy(0, rep, s).start()
    for s in range(parts):
        g_copy(1, rep, s).start()
    wacc[...] = lax.dot_general(
        agg[...], pre_grad, (((0,), (0,)), ((), ())), preferred_element_type=f32
    )
    half = wacc.shape[0] // 2
    strip = half // line

    def w_copy(step):
        src, dst, device = (
            (wcs, wcr, mate), (wys.at[1 - y], wyr, over), (wxs, wxr, across),
            (wfull.at[c, z, y], wfull.at[c, z, y], over), (wfull.at[c], wfull.at[c], mate),
        )[step]
        return remote(src, dst, w_send.at[step], w_recv.at[step], device)

    def w_arrival(step):
        dst = (wcr, wyr, wxr, wfull.at[c, z, 1 - y], wfull.at[1 - c])[step]
        remote(dst, dst, w_send.at[step], w_recv.at[step], mate).wait_recv()

    def wz_copy(k):
        other = (z + k) % line
        return remote(
            wzs.at[other], wzr.at[z], wz_send.at[k], wz_recv.at[z], (other * inner + x, rep)
        )

    def wz_wait(k):
        other = (z + k) % line
        remote(wzr.at[other], wzr.at[other], wz_send.at[k], wz_recv.at[other], across).wait_recv()

    def wa_copy(k):
        other = (z + k) % line
        here = wfull.at[c, z]
        return remote(here, here, wa_send.at[k], wa_recv.at[z], (other * inner + x, rep))

    def wa_wait(k):
        other = (z + k) % line
        there = wfull.at[c, other]
        remote(there, there, wa_send.at[k], wa_recv.at[other], across).wait_recv()

    def half_of(i):
        return pl.ds(pl.multiple_of(i * half, half), half)

    wcs[...] = wacc[half_of(1 - c), :].astype(bf16)
    w_copy(0).start()
    w_arrival(0)
    wzs[...] = (wacc[half_of(c), :] + wcr[...].astype(f32)).reshape(line, strip, width).astype(bf16)
    for k in range(1, line):
        wz_copy(k).start()

    def term_of(slot, s):
        return lax.dot_general(
            dense[slot], gbuf[s], (((0,), (0,)), ((), ())), preferred_element_type=f32
        )

    def x_copy(zz, s):
        return remote(xs.at[zz, s], xr.at[zz, s], x_send.at[zz, s], x_recv.at[zz, s], across)

    def send_across(s):
        @pl.loop(0, line)
        def _(i):
            d = line - 1 - i
            for zz, there in ((z + d, z + d < line), (z - d, (z - d >= 0) & (d > 0))):
                @pl.when(there)
                def _():
                    xs[zz, s] = term_of(zz * inner + 1 - x, s).astype(bf16)
                    x_copy(zz, s).start()

    def own_terms(s):
        @pl.loop(0, line)
        def _(zz):
            bown[zz, s] = term_of(zz * inner + x, s)

    def z_copy(zz, s, slot, device):
        return remote(zs.at[zz, s], zr.at[slot, s], z_send.at[zz, s], z_recv.at[slot, s], device)

    def z_wait(slot, s):
        remote(zr.at[slot, s], zr.at[slot, s], z_send.at[0, s], z_recv.at[slot, s], across).wait_recv()

    def pass_on(d, s):
        for zz, there, inflow, device, slot in (
            (z + d, z + d < line, z > 0, up, z + d),
            (z - d, z - d >= 0, z < line - 1, down, jnp.where(d == 1, line, z - d)),
        ):
            @pl.when(there)
            def _():
                x_copy(zz, s).wait_recv()
                bown[zz, s] += xr[zz, s].astype(f32)

                @pl.when(inflow)
                def _():
                    z_wait(zz, s)
                    bown[zz, s] += zr[zz, s].astype(f32)

                zs[zz, s] = bown[zz, s].astype(bf16)
                z_copy(zz, s, slot, device).start()

    def pass_rest(s):
        @pl.loop(1, line - 1)
        def _(i):
            pass_on(line - 1 - i, s)

    def finish(s):
        x_copy(z, s).wait_recv()
        bown[z, s] += xr[z, s].astype(f32)

        @pl.when(z > 0)
        def _():
            z_wait(z, s)
            bown[z, s] += zr[z, s].astype(f32)

        @pl.when(z < line - 1)
        def _():
            z_wait(line, s)
            bown[z, s] += zr[line, s].astype(f32)

        fg_out[:, s * cols:(s + 1) * cols] = bown[z, s].astype(bf16)

    def gather_grad(s):
        g_copy(1, y * 2 + 1 - c, s).wait_recv()
        g_copy(0, (1 - y) * 2 + c, s).wait_recv()
        g_copy(2, (1 - y) * 2 + c, s).start()

    def rest_of_grad(s):
        g_copy(2, (1 - y) * 2 + 1 - c, s).wait_recv()

    last = parts - 1
    for s in range(last):
        gather_grad(s)
        rest_of_grad(s)
        send_across(s)
        if s == 0:
            gather_grad(last)
        own_terms(s)
        pass_on(line - 1, s)
    for k in range(1, line):
        wz_wait(k)
    total = wzs[z].astype(f32)
    for k in range(1, line):
        total += wzr[(z + k) % line].astype(f32)
    wys[...] = total.reshape(2, strip // 2, width).astype(bf16)
    w_copy(1).start()
    rest_of_grad(last)
    w_arrival(1)
    wxs[...] = (wys[y].astype(f32) + wyr[...].astype(f32)).astype(bf16)
    w_copy(2).start()
    send_across(last)
    own_terms(last)
    for s in range(last):
        pass_rest(s)
    w_arrival(2)
    wfull[c, z, y] = ((wxs[...].astype(f32) + wxr[...].astype(f32)) * scale).astype(bf16)
    w_copy(3).start()
    for s in range(last):
        finish(s)
    pass_on(line - 1, last)
    w_arrival(3)
    for k in range(1, line):
        wa_copy(k).start()
    pass_rest(last)
    for k in range(1, line):
        wa_wait(k)
    w_copy(4).start()
    finish(last)
    w_arrival(4)
    wg_out[...] = wfull[...]

    @pl.loop(0, line)
    def _(zz):
        for s in range(parts):
            pl.when((zz < z) & (z < line - 1))(lambda: ag_copy(0, zz, s).wait_send())
            pl.when((zz > z) & (z > 0))(lambda: ag_copy(1, zz, s).wait_send())
            pl.when(zz != z)(lambda: ag_copy(2, zz, s).wait_send())
            x_copy(zz, s).wait_send()
            pl.when(zz != z)(lambda: z_copy(zz, s, zz, across).wait_send())
    for s in range(parts):
        y_copy(s).wait_send()
        for qy in range(2):
            c_copy(qy, s).wait_send()
        for way in range(3):
            g_copy(way, rep, s).wait_send()
    for step in range(5):
        w_copy(step).wait_send()
    for k in range(1, line):
        wz_copy(k).wait_send()
        wa_copy(k).wait_send()


def finish_kernel(a_ref, w_ref, f_ref, a_out, w_out, f_out):
    a_out[...] = a_ref[...]
    w_out[...] = w_ref[...].astype(jnp.float32)
    f_out[...] = f_ref[...]


def layer(features, hops, cotangent, weight, dense, scale, nodes):
    rows, width = features.shape
    inner = 2
    line = nodes // inner
    parts = 2
    cols = width // parts
    all_rows = dense.shape[1]
    half = width // 2
    strip = half // line
    bf16, f32, dma = jnp.bfloat16, jnp.float32, pltpu.SemaphoreType.DMA
    vmem = pl.BlockSpec(memory_space=pltpu.VMEM)
    shapes = [
        (dense.shape, bf16), ((nodes, parts, rows, cols), bf16), ((parts, all_rows, cols), f32),
        ((2, parts, rows, cols), bf16), ((2, parts, rows, cols), bf16),
        ((parts, rows, cols), bf16), ((parts, rows, cols), bf16),
        ((rows, width), bf16), ((parts, all_rows, cols), bf16), ((width, width), f32),
        ((half, width), bf16), ((half, width), bf16),
        ((strip // 2, width), bf16), ((strip // 2, width), bf16),
        ((2, strip // 2, width), bf16), ((strip // 2, width), bf16),
        ((line, strip, width), bf16), ((line, strip, width), bf16),
        ((2, line, 2, strip // 2, width), bf16),
        ((line, parts, rows, cols), f32), ((line, parts, rows, cols), bf16),
        ((line, parts, rows, cols), bf16), ((line, parts, rows, cols), bf16),
        ((line + 1, parts, rows, cols), bf16),
    ]
    sems = [
        dma, dma((3, line, parts)), dma((nodes, parts)), dma((2, parts)), dma((2, parts)),
        dma((parts,)), dma((parts,)), dma((3, parts)), dma((4, parts)), dma((5,)), dma((5,)),
        dma((line,)), dma((line,)), dma((line,)), dma((line,)),
        dma((line, parts)), dma((line, parts)), dma((line, parts)), dma((line + 1, parts)),
    ]
    held = sum(math.prod(shape) * jnp.dtype(kind).itemsize for shape, kind in shapes)
    activation, weight_grad, feature_grad = pl.pallas_call(
        functools.partial(layer_kernel, nodes, inner, scale),
        out_shape=(
            jax.ShapeDtypeStruct((rows, width), bf16),
            jax.ShapeDtypeStruct((2, line, 2, strip // 2, width), bf16),
            jax.ShapeDtypeStruct((rows, width), bf16),
        ),
        in_specs=[vmem] * 6 + [pl.BlockSpec(memory_space=pl.ANY)],
        out_specs=(vmem, vmem, vmem),
        scratch_shapes=[pltpu.VMEM(*shape) for shape in shapes] + sems,
        compiler_params=pltpu.CompilerParams(
            collective_id=0, has_side_effects=True, vmem_limit_bytes=min(held + (10 << 20), 63 << 20)
        ),
        name="layer",
    )(features, *hops, cotangent, weight, dense)
    return pl.pallas_call(
        finish_kernel,
        out_shape=(
            jax.ShapeDtypeStruct((rows, width), bf16),
            jax.ShapeDtypeStruct((width, width), f32),
            jax.ShapeDtypeStruct((rows, width), bf16),
        ),
        in_specs=[vmem] * 3,
        out_specs=(vmem, vmem, vmem),
        name="finish",
    )(activation, weight_grad.reshape(width, width), feature_grad)


def local(features, weight, cotangent, tile_values, tile_row, tile_col, tile_count):
    rows_quarter = features.shape[0]
    rep_count = lax.axis_size("rep")
    node_count = lax.axis_size("node")
    scale = 1.0 / math.sqrt(rows_quarter * rep_count * node_count)
    subs = rows_quarter // TB
    blocks = subs * rep_count
    inner = 2
    steps = (
        [(n, n ^ 1) for n in range(node_count)],
        [(n, n + inner) for n in range(node_count - inner)],
        [(n, n - inner) for n in range(inner, node_count)],
    )
    hops = [lax.ppermute(features, "node", step) for step in steps]
    dense = densify(tile_values, tile_row, tile_col, tile_count, node_count, blocks, subs)
    return layer(features, hops, cotangent, weight, dense, scale, node_count)


def solution(mesh):
    in_specs = (
        P(("node", "rep"), None),
        P(),
        P(("node", "rep"), None),
        P(("node", "rep"), None, None),
        P(("node", "rep")),
        P(("node", "rep")),
        P(("node", "rep")),
    )
    out_specs = (P(("node", "rep"), None), P(), P(("node", "rep"), None))
    return jax.shard_map(local, mesh=mesh, in_specs=in_specs, out_specs=out_specs, check_vma=False)
```

time: 101 us -> 102 us (level)
  starting transfers between devices: 0 us -> 7.94 us
  Pallas kernels: 93.5 us -> 87.9 us
  local copies, waits for them, and re-layouts: 5.6 us -> 4.36 us
    pallas_call x1, Pallas kernels: 84.3 us -> 75.2 us  [layer(): pl.pallas_call(functools.partial(layer_kernel, nodes, inner, scale), out_...]
    ppermute x0 -> x3, starting transfers between devices: none -> 7.94 us  [local(): hops = [lax.ppermute(features, 'node', step) for step in steps]]
    pallas_call x0 -> x1, Pallas kernels: none -> 2.4 us  [layer(): pl.pallas_call(finish_kernel, out_shape=(jax.ShapeDtypeStruct((rows, widt...]
    unnamed x3 -> x14, local copies, waits for them, and re-layouts: 5.6 us -> 4.36 us
    pallas_call x1, Pallas kernels: 9.19 us -> 10.3 us  [densify(): pl.pallas_call(functools.partial(densify_kernel, blocks, subs, group), ou...]
  transfers between devices with their start and end apart: 0 -> 3, of which waited for: 0 -> 0; matrix products, arithmetic and copies ran while one was open for 0% -> 0% of each run, Pallas kernels for 0% -> 10%
where the time goes in v3:
time: 102 us
  Pallas kernels  87.9 us (86%)
  starting transfers between devices  7.94 us (8%)
  local copies, waits for them, and re-layouts  4.36 us (4%)
  between operations  1.4 us (1%)
    pallas_call x1, Pallas kernels, layer(): pl.pallas_call(functools.partial(layer_kernel, nodes, inner, scale), out_...  75.2 us
    pallas_call x1, Pallas kernels, densify(): pl.pallas_call(functools.partial(densify_kernel, blocks, subs, group), ou...  10.3 us
    ppermute x3, starting transfers between devices, local(): hops = [lax.ppermute(features, 'node', step) for step in steps]  7.94 us
    unnamed x14, local copies, waits for them, and re-layouts  4.36 us
    pallas_call x1, Pallas kernels, layer(): pl.pallas_call(finish_kernel, out_shape=(jax.ShapeDtypeStruct((rows, widt...  2.4 us
  transfers between devices with their start and end apart: 3, of which 0 were waited for; matrix products, arithmetic and copies ran while one was open for 0% of the time, Pallas kernels for 10%

profile of v3, /device:TPU:0, one launch (start us, length us, event | category | flops | bytes accessed | tf_op | source)
XLA Modules:
  0.0 101.7 jit_solution(2485987625349829709)
XLA Ops:
  0.6 0.0 copy-start.3
  0.6 0.0 copy-start.4
  0.7 0.0 copy-start.1
  0.7 5.1 %collective-permute-start.1 = (bf16[256,512]{1,0:T(8,128)(2,1)}, bf16[256,512]{1,0:T(8,128)(2,1)S(1)}, u32[]{:S(2)}, u32[]{:S(2)}) collective-permute-start(bf16[256,512]{1,0:T(8,128)(2,1)} %feat.1), channel_id=1, source_target_pairs={{0,8},{4,12},{8,16},{12,20},{16,24},{20,28},{1,9},{5,13},{9,17},{1... | collective-permute-start | bytes 786440 | tf_op jit(solution)/shard_map/ppermute | solution.py:511
  5.8 1.6 %collective-permute-start = (bf16[256,512]{1,0:T(8,128)(2,1)}, bf16[256,512]{1,0:T(8,128)(2,1)S(1)}, u32[]{:S(2)}, u32[]{:S(2)}) collective-permute-start(bf16[256,512]{1,0:T(8,128)(2,1)} %feat.1), channel_id=1, source_target_pairs={{0,4},{4,0},{8,12},{12,8},{16,20},{20,16},{24,28},{28,24},{1,5},{5... | collective-permute-start | bytes 786440 | tf_op jit(solution)/shard_map/ppermute | solution.py:511
  7.3 1.3 %collective-permute-start.2 = (bf16[256,512]{1,0:T(8,128)(2,1)}, bf16[256,512]{1,0:T(8,128)(2,1)S(1)}, u32[]{:S(2)}, u32[]{:S(2)}) collective-permute-start(bf16[256,512]{1,0:T(8,128)(2,1)} %feat.1), channel_id=1, source_target_pairs={{8,0},{12,4},{16,8},{20,12},{24,16},{28,20},{9,1},{13,5},{17,9},{2... | collective-permute-start | bytes 786440 | tf_op jit(solution)/shard_map/ppermute | solution.py:511
  9.3 10.3 %densify.1.dense_hbm = bf16[8,1024,256]{2,1,0:T(8,128)(2,1)} custom-call(s32[256]{0:T(256)} %rows_ref.1, s32[256]{0:T(256)} %cols_ref.1, s32[1]{0:T(128)S(6)} %copy.10.count_ref, bf16[256,128,128]{2,1,0:T(8,128)(2,1)} %tiles_ref.1), custom_call_target="tpu_custom_call" | custom-call | flops 4194304 | bytes 16777216 | tf_op jit(solution)/shard_map/densify/pallas_call | solution.py:63
  19.6 0.0 collective-permute-done.1.feat_low
  19.6 0.0 collective-permute-done.feat_x
  19.6 0.0 collective-permute-done.2.feat_high
  19.6 0.0 copy-done.3
  19.6 0.0 copy-done.4
  19.6 0.0 copy-done.1
  19.6 0.0 copy-start
  19.7 2.2 %copy-done = bf16[8,1024,256]{2,1,0:T(8,128)(2,1)S(1)} copy-done((bf16[8,1024,256]{2,1,0:T(8,128)(2,1)S(1)}, bf16[8,1024,256]{2,1,0:T(8,128)(2,1)}, u32[]{:S(2)}) %copy-start) | copy-done | bytes 4194328
  21.8 75.2 %layer.1 = (bf16[256,512]{1,0:T(8,128)(2,1)S(1)}, bf16[2,4,2,32,512]{4,3,2,1,0:T(8,128)(2,1)S(1)}, bf16[256,512]{1,0:T(8,128)(2,1)S(1)}) custom-call(bf16[256,512]{1,0:T(8,128)(2,1)S(1)} %copy-done.3, bf16[256,512]{1,0:T(8,128)(2,1)S(1)} %collective-permute-done.feat_x, bf16[256,512]{1,0:T(8,128)(2,1)S(1)} %collective-permute-done.1.feat_low, ...), custom_call_target="tpu_custom_call" | custom-call | tf_op jit(solution)/shard_map/layer/pallas_call | solution.py:470
  97.1 0.0 copy-start.2
  97.1 0.8 copy-done.2
  97.9 0.0 copy-start.5
  97.9 0.7 copy-done.5
  98.6 0.0 copy-start.6
  98.6 0.7 copy-done.6
  99.2 2.4 %finish.1 = (bf16[256,512]{1,0:T(8,128)(2,1)}, f32[512,512]{1,0:T(8,128)}, bf16[256,512]{1,0:T(8,128)(2,1)}) custom-call(bf16[256,512]{1,0:T(8,128)(2,1)} %copy-done.5, bf16[512,512]{1,0:T(8,128)(2,1)} %bitcast.1, bf16[256,512]{1,0:T(8,128)(2,1)} %copy-done.6), custom_call_target="tpu_custom_call" | custom-call | tf_op jit(solution)/shard_map/finish/pallas_call | solution.py:485
Async XLA Ops:
  0.6 19.0 %copy-start.3 = (bf16[256,512]{1,0:T(8,128)(2,1)S(1)}, bf16[256,512]{1,0:T(8,128)(2,1)}, u32[]{:S(2)}) copy-start(bf16[256,512]{1,0:T(8,128)(2,1)} %feat.1) | copy-start | bytes 786436
  0.6 19.0 %copy-start.4 = (bf16[256,512]{1,0:T(8,128)(2,1)S(1)}, bf16[256,512]{1,0:T(8,128)(2,1)}, u32[]{:S(2)}) copy-start(bf16[256,512]{1,0:T(8,128)(2,1)} %cot.1) | copy-start | bytes 786436
  0.7 19.0 %copy-start.1 = (bf16[512,512]{1,0:T(8,128)(2,1)S(1)}, bf16[512,512]{1,0:T(8,128)(2,1)}, u32[]{:S(2)}) copy-start(bf16[512,512]{1,0:T(8,128)(2,1)} %weight.1) | copy-start | bytes 1572868
  0.7 18.9 %collective-permute-start.1 = (bf16[256,512]{1,0:T(8,128)(2,1)}, bf16[256,512]{1,0:T(8,128)(2,1)S(1)}, u32[]{:S(2)}, u32[]{:S(2)}) collective-permute-start(bf16[256,512]{1,0:T(8,128)(2,1)} %feat.1), channel_id=1, source_target_pairs={{0,8},{4,12},{8,16},{12,20},{16,24},{20,28},{1,9},{5,13},{9,17},{1... | collective-permute-start | bytes 786440 | tf_op jit(solution)/shard_map/ppermute | solution.py:511
  5.8 13.8 %collective-permute-start = (bf16[256,512]{1,0:T(8,128)(2,1)}, bf16[256,512]{1,0:T(8,128)(2,1)S(1)}, u32[]{:S(2)}, u32[]{:S(2)}) collective-permute-start(bf16[256,512]{1,0:T(8,128)(2,1)} %feat.1), channel_id=1, source_target_pairs={{0,4},{4,0},{8,12},{12,8},{16,20},{20,16},{24,28},{28,24},{1,5},{5... | collective-permute-start | bytes 786440 | tf_op jit(solution)/shard_map/ppermute | solution.py:511
  7.3 12.3 %collective-permute-start.2 = (bf16[256,512]{1,0:T(8,128)(2,1)}, bf16[256,512]{1,0:T(8,128)(2,1)S(1)}, u32[]{:S(2)}, u32[]{:S(2)}) collective-permute-start(bf16[256,512]{1,0:T(8,128)(2,1)} %feat.1), channel_id=1, source_target_pairs={{8,0},{12,4},{16,8},{20,12},{24,16},{28,20},{9,1},{13,5},{17,9},{2... | collective-permute-start | bytes 786440 | tf_op jit(solution)/shard_map/ppermute | solution.py:511
  19.6 2.2 %copy-start = (bf16[8,1024,256]{2,1,0:T(8,128)(2,1)S(1)}, bf16[8,1024,256]{2,1,0:T(8,128)(2,1)}, u32[]{:S(2)}) copy-start(bf16[8,1024,256]{2,1,0:T(8,128)(2,1)} %densify.1.dense_hbm) | copy-start | bytes 12582916
  97.1 0.8 copy-start.2
  97.9 0.7 copy-start.5
  98.6 0.7 copy-start.6

commit v4 on v3

--- a/solution.py
+++ b/solution.py
@@ -83,7 +83,7 @@
 
 
 def layer_kernel(
-    nodes, inner, scale, feat, feat_x, feat_low, feat_high, cot, weight, dense_hbm, act_out, wg_out, fg_out,
+    nodes, inner, scale, feat, cot, weight, dense_hbm, act_out, wg_out, fg_out,
     dense, xbuf, acc, cs, cr, ys, yr, agg, gbuf, wacc, wcs, wcr, wxs, wxr, wys, wyr, wzs, wzr, wfull,
     bown, xs, xr, zs, zr,
     dense_sem, ag_send, ag_recv, c_send, c_recv, y_send, y_recv, g_send, g_recv,
@@ -133,17 +133,10 @@
         return ref.at[:, s * cols:(s + 1) * cols]
 
     for s in range(parts):
-        low_part, high_part = columns(feat_low, s), columns(feat_high, s)
-
-        @pl.when(z > 0)
-        def _():
-            pl.when(z < line - 1)(lambda: ag_copy(0, z - 1, s, low_part).start())
-            ag_copy(2, z - 1, s, low_part).start()
-
-        @pl.when(z < line - 1)
-        def _():
-            pl.when(z > 0)(lambda: ag_copy(1, z + 1, s, high_part).start())
-            ag_copy(2, z + 1, s, high_part).start()
+        own = columns(feat, s)
+        ag_copy(2, z, s, own).start()
+        pl.when(z < line - 1)(lambda own=own, s=s: ag_copy(0, z, s, own).start())
+        pl.when(z > 0)(lambda own=own, s=s: ag_copy(1, z, s, own).start())
 
     load_dense.wait()
     chunk = rows
@@ -160,11 +153,8 @@
 
     for s in range(parts):
         multiply(node, s, columns(feat, s), True)
-        multiply(z * inner + 1 - x, s, columns(feat_x, s))
-        pl.when(z > 0)(lambda s=s: multiply(node - inner, s, columns(feat_low, s)))
-        pl.when(z < line - 1)(lambda s=s: multiply(node + inner, s, columns(feat_high, s)))
-
-    @pl.loop(2, line)
+
+    @pl.loop(1, line)
     def _(d):
         low, high = z - d, z + d
         for s in range(parts):
@@ -187,14 +177,14 @@
                     multiply(zz * inner + x, s, xbuf.at[zz * inner + x, s])
 
     def multiply_across(d, s):
-        for zz, there in ((z - d, z - d >= 0), (z + d, z + d < line)):
+        for zz, there in ((z - d, z - d >= 0), (z + d, (z + d < line) & (d > 0))):
             @pl.when(there)
             def _():
                 slot = zz * inner + 1 - x
                 ag_wait(slot, s)
                 multiply(slot, s, xbuf.at[slot, s])
 
-    @pl.loop(1, line - 1)
+    @pl.loop(0, line - 1)
     def _(d):
         for s in range(parts):
             multiply_across(d, s)
@@ -411,9 +401,9 @@
     @pl.loop(0, line)
     def _(zz):
         for s in range(parts):
-            pl.when((zz < z) & (z < line - 1))(lambda: ag_copy(0, zz, s).wait_send())
-            pl.when((zz > z) & (z > 0))(lambda: ag_copy(1, zz, s).wait_send())
-            pl.when(zz != z)(lambda: ag_copy(2, zz, s).wait_send())
+            pl.when((zz <= z) & (z < line - 1))(lambda: ag_copy(0, zz, s).wait_send())
+            pl.when((zz >= z) & (z > 0))(lambda: ag_copy(1, zz, s).wait_send())
+            ag_copy(2, zz, s).wait_send()
             x_copy(zz, s).wait_send()
             pl.when(zz != z)(lambda: z_copy(zz, s, zz, across).wait_send())
     for s in range(parts):
@@ -435,7 +425,7 @@
     f_out[...] = f_ref[...]
 
 
-def layer(features, hops, cotangent, weight, dense, scale, nodes):
+def layer(features, cotangent, weight, dense, scale, nodes):
     rows, width = features.shape
     inner = 2
     line = nodes // inner
@@ -466,7 +456,6 @@
         dma((line,)), dma((line,)), dma((line,)), dma((line,)),
         dma((line, parts)), dma((line, parts)), dma((line, parts)), dma((line + 1, parts)),
     ]
-    held = sum(math.prod(shape) * jnp.dtype(kind).itemsize for shape, kind in shapes)
     activation, weight_grad, feature_grad = pl.pallas_call(
         functools.partial(layer_kernel, nodes, inner, scale),
         out_shape=(
@@ -474,14 +463,14 @@
             jax.ShapeDtypeStruct((2, line, 2, strip // 2, width), bf16),
             jax.ShapeDtypeStruct((rows, width), bf16),
         ),
-        in_specs=[vmem] * 6 + [pl.BlockSpec(memory_space=pl.ANY)],
+        in_specs=[vmem] * 3 + [pl.BlockSpec(memory_space=pl.ANY)],
         out_specs=(vmem, vmem, vmem),
         scratch_shapes=[pltpu.VMEM(*shape) for shape in shapes] + sems,
         compiler_params=pltpu.CompilerParams(
-            collective_id=0, has_side_effects=True, vmem_limit_bytes=min(held + (10 << 20), 63 << 20)
+            collective_id=0, has_side_effects=True, vmem_limit_bytes=63 << 20
         ),
         name="layer",
-    )(features, *hops, cotangent, weight, dense)
+    )(features, cotangent, weight, dense)
     return pl.pallas_call(
         finish_kernel,
         out_shape=(
@@ -502,15 +491,8 @@
     scale = 1.0 / math.sqrt(rows_quarter * rep_count * node_count)
     subs = rows_quarter // TB
     blocks = subs * rep_count
-    inner = 2
-    steps = (
-        [(n, n ^ 1) for n in range(node_count)],
-        [(n, n + inner) for n in range(node_count - inner)],
-        [(n, n - inner) for n in range(inner, node_count)],
-    )
-    hops = [lax.ppermute(features, "node", step) for step in steps]
     dense = densify(tile_values, tile_row, tile_col, tile_count, node_count, blocks, subs)
-    return layer(features, hops, cotangent, weight, dense, scale, node_count)
+    return layer(features, cotangent, weight, dense, scale, node_count)
 
 
 def solution(mesh):

time: 102 us -> 101 us (level)
  Pallas kernels: 87.9 us -> 99.2 us
  starting transfers between devices: 7.94 us -> 0 us
  local copies, waits for them, and re-layouts: 4.36 us -> 0 us
    pallas_call x1, Pallas kernels: 75.2 us -> 86.9 us  [layer(): pl.pallas_call(functools.partial(layer_kernel, nodes, inner, scale), out_...]
    ppermute x3 -> x0, starting transfers between devices: 7.94 us -> none  [local(): hops = [lax.ppermute(features, 'node', step) for step in steps]]
    unnamed x14 -> x0, local copies, waits for them, and re-layouts: 4.36 us -> none
  transfers between devices with their start and end apart: 3 -> 0, of which waited for: 0 -> 0; matrix products, arithmetic and copies ran while one was open for 0% -> 0% of each run, Pallas kernels for 10% -> 0%
where the time goes in v4:
time: 101 us; the launch traced here: 100 us
  Pallas kernels  99.2 us (98%)
  between operations  1.29 us (1%)
    pallas_call x1, Pallas kernels, layer(): pl.pallas_call(functools.partial(layer_kernel, nodes, inner, scale), out_...  86.9 us
    pallas_call x1, Pallas kernels, densify(): pl.pallas_call(functools.partial(densify_kernel, blocks, subs, group), ou...  9.88 us
    pallas_call x1, Pallas kernels, layer(): pl.pallas_call(finish_kernel, out_shape=(jax.ShapeDtypeStruct((rows, widt...  2.41 us

profile of v4, /device:TPU:0, one launch (start us, length us, event | category | flops | bytes accessed | tf_op | source)
XLA Modules:
  0.0 100.5 jit_solution(12420186153643547099)
XLA Ops:
  1.3 9.9 %densify.1.dense_hbm = bf16[8,1024,256]{2,1,0:T(8,128)(2,1)} custom-call(s32[256]{0:T(256)} %rows_ref.1, s32[256]{0:T(256)} %cols_ref.1, s32[1]{0:T(128)S(6)} %copy.10.count_ref, bf16[256,128,128]{2,1,0:T(8,128)(2,1)} %tiles_ref.1), custom_call_target="tpu_custom_call" | custom-call | flops 4194304 | bytes 16777216 | tf_op jit(solution)/shard_map/densify/pallas_call | solution.py:63
  11.2 86.9 %layer.1 = (bf16[256,512]{1,0:T(8,128)(2,1)}, bf16[2,4,2,32,512]{4,3,2,1,0:T(8,128)(2,1)}, bf16[256,512]{1,0:T(8,128)(2,1)}) custom-call(bf16[256,512]{1,0:T(8,128)(2,1)} %feat.1, bf16[256,512]{1,0:T(8,128)(2,1)} %cot.1, bf16[512,512]{1,0:T(8,128)(2,1)} %weight.1, bf16[8,1024,256]{2,1,0:T(8,128)(2,1)} %densify.1.dense_hbm), custom_call_target="tpu_custom_call" | custom-call | tf_op jit(solution)/shard_map/layer/pallas_call | solution.py:459
  98.1 2.4 %finish.1 = (bf16[256,512]{1,0:T(8,128)(2,1)}, f32[512,512]{1,0:T(8,128)}, bf16[256,512]{1,0:T(8,128)(2,1)}) custom-call(bf16[256,512]{1,0:T(8,128)(2,1)} %get-tuple-element.6.a_ref, bf16[512,512]{1,0:T(8,128)(2,1)} %bitcast.1, bf16[256,512]{1,0:T(8,128)(2,1)} %get-tuple-element.8.f_ref), custom_call_target="tpu_custom_call" | custom-call | tf_op jit(solution)/shard_map/finish/pallas_call | solution.py:474

commit v5 on v4

--- a/solution.py
+++ b/solution.py
@@ -84,7 +84,7 @@
 
 def layer_kernel(
     nodes, inner, scale, feat, cot, weight, dense_hbm, act_out, wg_out, fg_out,
-    dense, xbuf, acc, cs, cr, ys, yr, agg, gbuf, wacc, wcs, wcr, wxs, wxr, wys, wyr, wzs, wzr, wfull,
+    dense, turned, xbuf, acc, cs, cr, ys, yr, agg, gbuf, wacc, wcs, wcr, wxs, wxr, wys, wyr, wzs, wzr, wfull,
     bown, xs, xr, zs, zr,
     dense_sem, ag_send, ag_recv, c_send, c_recv, y_send, y_recv, g_send, g_recv,
     w_send, w_recv, wz_send, wz_recv, wa_send, wa_recv, x_send, x_recv, z_send, z_recv,
@@ -206,6 +206,15 @@
         c_copy(1 - y, s).wait_recv()
         ys[s] = (acc[s, quarter((1 - y) * 2 + c), :] + cr[1 - y, s].astype(f32)).astype(bf16)
         y_copy(s).start()
+    turned_ready = turned.shape[0] == nodes
+
+    def turn(side):
+        if turned_ready:
+            @pl.loop(0, line)
+            def _(zz):
+                turned[zz * inner + side] = dense[zz * inner + side].T
+
+    turn(1 - x)
     for s in range(parts):
         c_copy(y, s).wait_recv()
         y_copy(s).wait_recv()
@@ -281,7 +290,11 @@
     for k in range(1, line):
         wz_copy(k).start()
 
+    turn(x)
+
     def term_of(slot, s):
+        if turned_ready:
+            return jnp.dot(turned[slot], gbuf[s], preferred_element_type=f32)
         return lax.dot_general(
             dense[slot], gbuf[s], (((0,), (0,)), ((), ())), preferred_element_type=f32
         )
@@ -436,8 +449,9 @@
     strip = half // line
     bf16, f32, dma = jnp.bfloat16, jnp.float32, pltpu.SemaphoreType.DMA
     vmem = pl.BlockSpec(memory_space=pltpu.VMEM)
+    flipped = (nodes, dense.shape[2], all_rows) if dense.size < 4 << 20 else (1, 16, 128)
     shapes = [
-        (dense.shape, bf16), ((nodes, parts, rows, cols), bf16), ((parts, all_rows, cols), f32),
+        (dense.shape, bf16), (flipped, bf16), ((nodes, parts, rows, cols), bf16), ((parts, all_rows, cols), f32),
         ((2, parts, rows, cols), bf16), ((2, parts, rows, cols), bf16),
         ((parts, rows, cols), bf16), ((parts, rows, cols), bf16),
         ((rows, width), bf16), ((parts, all_rows, cols), bf16), ((width, width), f32),

time: 101 us -> 99.9 us (0.989)
  Pallas kernels: 99.2 us -> 97.9 us
    pallas_call x1, Pallas kernels: 86.9 us -> 85.2 us  [layer(): pl.pallas_call(functools.partial(layer_kernel, nodes, inner, scale), out_...]
where the time goes in v5:
time: 99.9 us; the launch traced here: 99.2 us
  Pallas kernels  97.9 us (98%)
  between operations  1.29 us (1%)
    pallas_call x1, Pallas kernels, layer(): pl.pallas_call(functools.partial(layer_kernel, nodes, inner, scale), out_...  85.2 us
    pallas_call x1, Pallas kernels, densify(): pl.pallas_call(functools.partial(densify_kernel, blocks, subs, group), ou...  10.3 us
    pallas_call x1, Pallas kernels, layer(): pl.pallas_call(finish_kernel, out_shape=(jax.ShapeDtypeStruct((rows, widt...  2.41 us

profile of v5, /device:TPU:0, one launch (start us, length us, event | category | flops | bytes accessed | tf_op | source)
XLA Modules:
  0.0 99.2 jit_solution(1433903730019714646)
XLA Ops:
  1.3 10.3 %densify.1.dense_hbm = bf16[8,1024,256]{2,1,0:T(8,128)(2,1)} custom-call(s32[256]{0:T(256)} %rows_ref.1, s32[256]{0:T(256)} %cols_ref.1, s32[1]{0:T(128)S(6)} %copy.10.count_ref, bf16[256,128,128]{2,1,0:T(8,128)(2,1)} %tiles_ref.1), custom_call_target="tpu_custom_call" | custom-call | flops 4194304 | bytes 16777216 | tf_op jit(solution)/shard_map/densify/pallas_call | solution.py:63
  11.6 85.2 %layer.1 = (bf16[256,512]{1,0:T(8,128)(2,1)}, bf16[2,4,2,32,512]{4,3,2,1,0:T(8,128)(2,1)}, bf16[256,512]{1,0:T(8,128)(2,1)}) custom-call(bf16[256,512]{1,0:T(8,128)(2,1)} %feat.1, bf16[256,512]{1,0:T(8,128)(2,1)} %cot.1, bf16[512,512]{1,0:T(8,128)(2,1)} %weight.1, bf16[8,1024,256]{2,1,0:T(8,128)(2,1)} %densify.1.dense_hbm), custom_call_target="tpu_custom_call" | custom-call | tf_op jit(solution)/shard_map/layer/pallas_call | solution.py:473
  96.8 2.4 %finish.1 = (bf16[256,512]{1,0:T(8,128)(2,1)}, f32[512,512]{1,0:T(8,128)}, bf16[256,512]{1,0:T(8,128)(2,1)}) custom-call(bf16[256,512]{1,0:T(8,128)(2,1)} %get-tuple-element.6.a_ref, bf16[512,512]{1,0:T(8,128)(2,1)} %bitcast.1, bf16[256,512]{1,0:T(8,128)(2,1)} %get-tuple-element.8.f_ref), custom_call_target="tpu_custom_call" | custom-call | tf_op jit(solution)/shard_map/finish/pallas_call | solution.py:488
